TPU v7x, 32 devices: a whole 2x2x4 slice. The times are simulated.
32 devices in a mesh: task: 4 (over z), feat: 8 (over y, x, core).
Axes of the slice: x: 2, y: 2, z: 4, core: 2. Of those that a mesh axis runs over, the one named last changes fastest.
Arguments:
- inputs: bfloat16 [4, 64, 512, 512], P('task', 'feat'), may hold values from -6 to 6
- context: int32 [4], P('task'), may hold values from 50 to 500, as said below
- sample_mask: int32 [4, 512], P('task'), may hold values from 0 to 1, as said below
- sample_gain: float32 [512], replicated, may hold values from 0.5 to 1.5
- sample_shift: float32 [512], replicated, may hold values from -2 to 2
- sample_project: bfloat16 [512, 1536], replicated, may hold values from -0.25 to 0.25
- sample_output: bfloat16 [512, 512], replicated, may hold values from -1 to 1
- sample_bias: float32 [512], replicated, may hold values from -2 to 2
- feature_gain: float32 [512], replicated, may hold values from 0.5 to 1.5
- feature_shift: float32 [512], replicated, may hold values from -2 to 2
- feature_project: bfloat16 [512, 1536], replicated, may hold values from -0.25 to 0.25
- feature_output: bfloat16 [512, 512], replicated, may hold values from -0.75 to 0.75
- feature_bias: float32 [512], replicated, may hold values from -2 to 2
- dense_gain: float32 [512], replicated, may hold values from 0.5 to 1.5
- dense_shift: float32 [512], replicated, may hold values from -2 to 2
- up_weight: bfloat16 [512, 2048], replicated, may hold values from -0.25 to 0.25
- up_bias: float32 [2048], replicated, may hold values from -2 to 2
- down_weight: bfloat16 [2048, 512], replicated, may hold values from -0.125 to 0.125
- down_bias: float32 [512], replicated, may hold values from -2 to 2
- cotangent: bfloat16 [4, 64, 512, 512], P('task', 'feat'), may hold values from -6 to 6
Outputs:
- output: bfloat16 [4, 64, 512, 512], P('task', 'feat')
- input_grad: float32 [4, 64, 512, 512], P('task', 'feat')
- sample_gain_grad: float32 [512], replicated
- sample_shift_grad: float32 [512], replicated
- sample_project_grad: float32 [512, 1536], replicated
- sample_output_grad: float32 [512, 512], replicated
- sample_bias_grad: float32 [512], replicated
- feature_gain_grad: float32 [512], replicated
- feature_shift_grad: float32 [512], replicated
- feature_project_grad: float32 [512, 1536], replicated
- feature_output_grad: float32 [512, 512], replicated
- feature_bias_grad: float32 [512], replicated
- dense_gain_grad: float32 [512], replicated
- dense_shift_grad: float32 [512], replicated
- up_weight_grad: float32 [512, 2048], replicated
- up_bias_grad: float32 [2048], replicated
- down_weight_grad: float32 [2048, 512], replicated
- down_bias_grad: float32 [512], replicated
Inputs may be any that keep to these rules, and one draw needn't show every extreme that they name: In every draw one task has context 50 and another 500. `sample_mask`: sample 0 of every task is present.
All inputs are finite; a program needn't handle non-finite values.
Results may differ from a plain program's by a relative error of at most 0.015.
Values may be sent and summed in bfloat16 or wider, within the bound.
A program may use at most 384 MiB of HBM per device.

v0:
```python
import functools
import math

import jax
import jax.numpy as jnp
from jax import lax
from jax.experimental import pallas as pl
from jax.experimental.pallas import tpu as pltpu
from jax.sharding import PartitionSpec as P

HEADS = 8
HEAD = 64
PAIR = 2 * HEAD
EPSILON = 1e-05
SCALE = HEAD ** (-0.5)
POWER = SCALE * math.log2(math.e)
MASKED = -1e30
GELU_A = math.sqrt(2.0 / math.pi)
GELU_B = 0.044715
BF = jnp.bfloat16
F32 = jnp.float32
LIMIT = 60 * 1024 * 1024
MESH = pl.DeviceIdType.MESH


def dot(left, right, left_dim, right_dim):
    return lax.dot_general(
        left, right, (((left_dim,), (right_dim,)), ((), ())), preferred_element_type=F32
    )


def normalize(rows):
    center = rows - jnp.mean(rows, axis=-1, keepdims=True)
    spread = jnp.mean(center * center, axis=-1, keepdims=True)
    inverse = lax.rsqrt(spread + EPSILON)
    return center * inverse, inverse


def normalize_back(grad_normed, gain, hat, inverse):
    scaled = grad_normed * gain
    middle = jnp.mean(scaled, axis=-1, keepdims=True)
    along = jnp.mean(scaled * hat, axis=-1, keepdims=True)
    grad_rows = inverse * (scaled - middle - hat * along)
    grad_gain = jnp.sum(grad_normed * hat, axis=0, keepdims=True)
    grad_shift = jnp.sum(grad_normed, axis=0, keepdims=True)
    return grad_rows, grad_gain, grad_shift


def pieces(row):
    high = row.astype(BF).astype(F32)
    rest = row - high
    middle = rest.astype(BF).astype(F32)
    return high, middle, rest - middle


def extra_rows(count, width, rows):
    place = lax.broadcasted_iota(jnp.int32, (16, width), 0)
    block = jnp.zeros((16, width), F32)
    for index, row in enumerate(rows):
        block = jnp.where(place == index, row, block)
    return jnp.concatenate([block.astype(BF), jnp.zeros((HEAD - 16, width), BF)], axis=0)


def half_ones(odd, depth):
    lane = lax.broadcasted_iota(jnp.int32, (depth, PAIR), 1)
    own = (lane >= HEAD) if odd else (lane < HEAD)
    return own.astype(F32).astype(BF)


def stack_half(odd, own, extra):
    return jnp.concatenate([extra, own] if odd else [own, extra], axis=0)


def extra_columns(odd, depth, columns):
    lane = lax.broadcasted_iota(jnp.int32, (depth, PAIR), 1)
    first = 0 if odd else HEAD
    block = jnp.zeros((depth, PAIR), F32)
    for index, column in enumerate(columns):
        block = jnp.where(lane == first + index, column, block)
    return block.astype(BF)


def attend_head(keys, left_extra, own, query_rows, extra, odd, value_rows):
    left = keys * own + left_extra
    scores = dot(left, stack_half(odd, query_rows, extra), 1, 0)
    highest = jnp.max(scores, axis=0, keepdims=True)
    weights = jnp.exp2((scores - highest) * POWER)
    totals = jnp.sum(weights, axis=0, keepdims=True)
    mixed = dot(value_rows, weights.astype(BF), 1, 0) / totals
    log_total = highest + jnp.log2(totals) * (1.0 / POWER)
    return mixed, log_total


def attend_head_back(left, right, value_left, value_right, query_rows, key_rows, grad_rows):
    shares = jnp.exp2(dot(left, right, 1, 0) * POWER)
    grad_shares = dot(value_left, value_right, 1, 0)
    low_scores = (shares * grad_shares).astype(BF)
    grad_values = dot(grad_rows, shares.astype(BF), 1, 1)
    grad_keys = dot(query_rows, low_scores, 1, 1) * SCALE
    grad_queries = dot(key_rows, low_scores, 1, 0) * SCALE
    return grad_queries, grad_keys, grad_values


def push(source, target, send_sem, recv_sem, peer):
    return pltpu.make_async_remote_copy(
        src_ref=source, dst_ref=target, send_sem=send_sem, recv_sem=recv_sem,
        device_id={"feat": peer}, device_id_type=MESH,
    )


def greet(peers, me):
    barrier = pltpu.get_barrier_semaphore()
    for hop in range(1, peers):
        pl.semaphore_signal(
            barrier, inc=1, device_id={"feat": (me + hop) % peers}, device_id_type=MESH
        )
    pl.semaphore_wait(barrier, peers - 1)


def arrived(buffer, sem):
    pltpu.make_async_copy(buffer, buffer, sem).wait()


def sample_forward_kernel(
    peers,
    inputs_ref, mask_ref, gain_ref, shift_ref, query_w, key_w, value_w, output_w, bias_ref,
    seen_ref, saved_ref, mixed_ref, log_ref,
    outbox, send_sems, recv_sems, own_sems,
):
    step = pl.program_id(0)
    steps = pl.num_programs(0)
    slot = step % 2
    me = lax.axis_index("feat")

    @pl.when(step == 0)
    def _():
        greet(peers, me)

    def moves(at, slot):
        sends = []
        for hop in range(1, peers):
            peer = (me + hop) % peers
            sends.append(
                push(
                    outbox.at[slot, peer], seen_ref.at[me, at],
                    send_sems.at[slot, hop], recv_sems.at[hop], peer,
                )
            )
        own = pltpu.make_async_copy(outbox.at[slot, me], seen_ref.at[me, at], own_sems.at[slot])
        return sends, own

    def drain(at, slot):
        sends, own = moves(at, slot)
        for send in sends:
            send.wait_send()
        own.wait()

    rows = inputs_ref[0].astype(F32)
    samples, width = rows.shape
    hat, _ = normalize(rows)
    normed = (hat * gain_ref[...] + shift_ref[...]).astype(BF)
    saved_ref[0, 0] = dot(query_w[...], normed, 1, 1).astype(BF)
    saved_ref[0, 1] = dot(normed, key_w[...], 1, 0).astype(BF)
    saved_ref[0, 2] = dot(value_w[...], normed, 1, 1).astype(BF)
    mask = mask_ref[...]
    extra = extra_rows(1, samples, [jnp.ones((1, samples), F32)])
    for odd in (False, True):
        own = half_ones(odd, samples)
        left_extra = extra_columns(odd, samples, [mask])
        for pair in range(width // PAIR):
            head = 2 * pair + odd
            first = head * HEAD
            mixed, log_total = attend_head(
                saved_ref[0, 1, :, pair * PAIR:(pair + 1) * PAIR], left_extra, own,
                saved_ref[0, 0, first:first + HEAD, :], extra, odd,
                saved_ref[0, 2, first:first + HEAD, :],
            )
            mixed_ref[0, first:first + HEAD, :] = mixed.astype(BF)
            log_ref[0, head:head + 1, :] = log_total
    branch = dot(mixed_ref[0], output_w[...], 0, 0) + bias_ref[...]
    after = (inputs_ref[0].astype(F32) + branch).astype(BF)

    @pl.when(step >= 2)
    def _():
        drain(step - 2, slot)

    outbox[slot] = after.reshape(outbox.shape[1:])
    sends, own = moves(step, slot)
    for send in sends:
        send.start()
    own.start()

    @pl.when(step == steps - 1)
    def _():
        drain(step, slot)
        if seen_ref.shape[1] > 1:
            drain(step - 1, 1 - slot)
        for hop in range(1, peers):
            arrived(seen_ref.at[(me + peers - hop) % peers], recv_sems.at[hop])


def sample_backward_kernel(
    inputs_ref, mask_ref, gain_ref, shift_ref, project_t, output_w,
    saved_ref, mixed_ref, log_ref, grad_ref, result_ref,
    input_grad_ref, final_ref, project_grad, output_grad, vector_grad,
    project_sum, output_sum, packed_grad,
):
    step = pl.program_id(0)

    @pl.when(step == 0)
    def _():
        project_sum[...] = jnp.zeros_like(project_sum)
        output_sum[...] = jnp.zeros_like(output_sum)
        vector_grad[...] = jnp.zeros_like(vector_grad)

    samples, width = inputs_ref.shape[1:]
    final_ref[0] = result_ref[...].reshape(samples, width)
    low_grad = grad_ref[...].reshape(samples, width)
    output_sum[...] += dot(mixed_ref[0], low_grad, 1, 0)
    grad_mixed = dot(output_w[...], low_grad, 1, 1)
    low_mixed = grad_mixed.astype(BF)
    delta = (low_mixed.astype(F32) * mixed_ref[0].astype(F32))
    delta = jnp.sum(delta.reshape(width // HEAD, HEAD, samples), axis=1)
    mask = mask_ref[...]
    ones = jnp.ones((samples, 1), F32)
    one_row = jnp.ones((1, samples), F32)
    for odd in (False, True):
        own = half_ones(odd, samples)
        key_extra = extra_columns(odd, samples, [mask, ones, ones, ones])
        value_extra = extra_columns(odd, samples, [ones, ones, ones])
        for pair in range(width // PAIR):
            head = 2 * pair + odd
            first = head * HEAD
            lanes = slice(pair * PAIR, (pair + 1) * PAIR)
            query_rows = saved_ref[0, 0, first:first + HEAD, :]
            value_rows = saved_ref[0, 2, first:first + HEAD, :]
            grad_rows = low_mixed[first:first + HEAD, :]
            keys = saved_ref[0, 1, :, lanes]
            key_rows = keys.T[HEAD:] if odd else keys.T[:HEAD]
            high, middle, low = pieces(-log_ref[0, head:head + 1, :])
            right = stack_half(odd, query_rows, extra_rows(4, samples, [one_row, high, middle, low]))
            high, middle, low = pieces(-delta[head:head + 1, :])
            value_right = jnp.concatenate(
                [grad_rows, extra_rows(3, samples, [high, middle, low])], axis=0
            )
            value_left = jnp.concatenate(
                [value_rows, extra_rows(3, samples, [one_row] * 3)], axis=0
            )
            shares = jnp.exp2(dot(keys * own + key_extra, right, 1, 0) * POWER)
            grad_shares = dot(value_left, value_right, 0, 0)
            low_scores = (shares * grad_shares).astype(BF)
            packed_grad[2 * width + first:2 * width + first + HEAD, :] = dot(
                grad_rows, shares.astype(BF), 1, 1
            ).astype(BF)
            packed_grad[width + first:width + first + HEAD, :] = (
                dot(query_rows, low_scores, 1, 1) * SCALE
            ).astype(BF)
            packed_grad[first:first + HEAD, :] = (
                dot(key_rows, low_scores, 1, 0) * SCALE
            ).astype(BF)
    hat, inverse = normalize(inputs_ref[0].astype(F32))
    normed = (hat * gain_ref[...] + shift_ref[...]).astype(BF)
    project_sum[...] += dot(packed_grad[...], normed, 1, 0)
    grad_normed = dot(packed_grad[...], project_t[...], 0, 0)
    grad_rows, grad_gain, grad_shift = normalize_back(grad_normed, gain_ref[...], hat, inverse)
    stream = low_grad.astype(F32)
    input_grad_ref[0] = stream + grad_rows
    vector_grad[0:1, :] += grad_gain
    vector_grad[1:2, :] += grad_shift
    vector_grad[2:3, :] += jnp.sum(stream, axis=0, keepdims=True)

    @pl.when(step == pl.num_programs(0) - 1)
    def _():
        project_grad[...] = project_sum[...].T.astype(BF)
        output_grad[...] = output_sum[...].astype(BF)


def to_groups(block_ref, spare):
    features, group, width = block_ref.shape
    rows = block_ref[...].astype(F32).reshape(features * group, width)
    columns = []
    for lanes in range(width // 128):
        spare[lanes] = rows[:, lanes * 128:(lanes + 1) * 128]
        columns.append(
            jnp.concatenate(
                [spare[lanes, pl.ds(one, features, stride=group), :] for one in range(group)],
                axis=0,
            )
        )
    return jnp.concatenate(columns, axis=1)


def from_groups(rows, block_ref, spare):
    features, group, width = block_ref.shape
    for lanes in range(width // 128):
        span = slice(lanes * 128, (lanes + 1) * 128)
        for one in range(group):
            spare[lanes, pl.ds(one, features, stride=group), :] = rows[
                one * features:(one + 1) * features, span
            ]
        block_ref[:, :, span] = spare[lanes].reshape(features, group, 128).astype(BF)


def feature_kernel(
    peers,
    stream_ref, cotangent_hbm, gain_ref, shift_ref, query_w, key_w, value_w, project_t, output_w,
    bias_ref, dense_gain_ref, dense_shift_ref, up_ref, up_bias_ref, down_ref, down_bias_ref,
    results_ref, grads_ref, project_grad, output_grad, up_grad, down_grad, vector_grad, hidden_grad,
    project_sum, output_sum, up_sum, down_sum, spare, query_t, keys_s, value_t, mixed_t, logs,
    packed_grad, cotangents, result_box, grad_box,
    cotangent_sends, cotangent_recvs, result_sends, grad_sends, result_recvs, grad_recvs, own_sems,
):
    step = pl.program_id(0)
    steps, features, group, _ = cotangents.shape
    slot = step % 2
    me = lax.axis_index("feat")
    local = features // peers
    share = steps * group
    chunks, width, chunk = up_ref.shape
    tokens = features * group
    joined = 2 * features

    def cotangent_moves(at, own=False):
        def part(peer):
            return cotangent_hbm.at[:, pl.ds(pl.multiple_of(peer * share + at * group, group), group), :]

        inbox = cotangents.at[at, pl.ds(me * local, local)]
        if own:
            return pltpu.make_async_copy(part(me), inbox, cotangent_recvs.at[at])
        sends = []
        for hop in range(1, peers):
            peer = (me + hop) % peers
            sends.append(
                push(part(peer), inbox, cotangent_sends.at[at % 2, hop], cotangent_recvs.at[at], peer)
            )
        return sends

    def start_cotangent(at):
        for send in cotangent_moves(at):
            send.start()
        cotangent_moves(at, own=True).start()

    def back_moves(at, slot, box, target, send_sems, recv_sems, own_sem):
        place = target.at[me, :, pl.ds(pl.multiple_of(at * group, group), group), :]
        sends = []
        for hop in range(1, peers):
            peer = (me + hop) % peers
            sends.append(
                push(
                    box.at[slot, pl.ds(peer * local, local)], place,
                    send_sems.at[slot, hop], recv_sems.at[hop], peer,
                )
            )
        own = pltpu.make_async_copy(box.at[slot, pl.ds(me * local, local)], place, own_sem)
        return sends, own

    def result_moves(at, slot):
        return back_moves(
            at, slot, result_box, results_ref, result_sends, result_recvs, own_sems.at[0, slot]
        )

    def grad_moves(at, slot):
        return back_moves(
            at, slot, grad_box, grads_ref, grad_sends, grad_recvs, own_sems.at[1, slot]
        )

    def begin(moves):
        sends, own = moves
        for send in sends:
            send.start()
        own.start()

    def drain(moves):
        sends, own = moves
        for send in sends:
            send.wait_send()
        own.wait()

    @pl.when(step == 0)
    def _():
        greet(peers, me)
        start_cotangent(0)

    @pl.when(step + 1 < steps)
    def _():
        @pl.when(step >= 1)
        def _():
            for send in cotangent_moves(step - 1):
                send.wait_send()

        start_cotangent(step + 1)

    @pl.when(step == 0)
    def _():
        project_sum[...] = jnp.zeros_like(project_sum)
        output_sum[...] = jnp.zeros_like(output_sum)
        up_sum[...] = jnp.zeros_like(up_sum)
        down_sum[...] = jnp.zeros_like(down_sum)
        vector_grad[...] = jnp.zeros_like(vector_grad)
        hidden_grad[...] = jnp.zeros_like(hidden_grad)

    rows = to_groups(stream_ref, spare)
    hat, inverse = normalize(rows)
    normed = (hat * gain_ref[...] + shift_ref[...]).astype(BF)
    query_t[...] = dot(query_w[...], normed, 1, 1).astype(BF)
    keys_s[...] = dot(normed, key_w[...], 1, 0).astype(BF)
    value_t[...] = dot(value_w[...], normed, 1, 1).astype(BF)
    place = lax.broadcasted_iota(jnp.int32, (joined, 1), 0)
    place_row = lax.broadcasted_iota(jnp.int32, (1, joined), 1)
    key_first = (place < features).astype(F32)
    key_second = (place >= features).astype(F32)
    hide_first = jnp.where(place_row >= features, MASKED, 0.0)
    hide_second = jnp.where(place_row < features, MASKED, 0.0)
    ones = jnp.ones((joined, 1), F32)
    one_row = jnp.ones((1, joined), F32)
    extra = extra_rows(2, joined, [hide_first, hide_second])
    for odd in (False, True):
        own = half_ones(odd, joined)
        left_extra = extra_columns(odd, joined, [key_first, key_second])
        for pair in range(width // PAIR):
            head = 2 * pair + odd
            first = head * HEAD
            for part in range(tokens // joined):
                span = slice(part * joined, (part + 1) * joined)
                mixed, log_total = attend_head(
                    keys_s[span, pair * PAIR:(pair + 1) * PAIR], left_extra, own,
                    query_t[first:first + HEAD, span], extra, odd,
                    value_t[first:first + HEAD, span],
                )
                mixed_t[first:first + HEAD, span] = mixed.astype(BF)
                logs[head:head + 1, span] = log_total
    after = rows + dot(mixed_t[...], output_w[...], 0, 0) + bias_ref[...]

    dense_hat, dense_inverse = normalize(after)
    dense_in = (dense_hat * dense_gain_ref[...] + dense_shift_ref[...]).astype(BF)
    arrived(cotangents.at[step], cotangent_recvs.at[step])
    stream = to_groups(cotangents.at[step], spare)
    low_stream = stream.astype(BF)
    result = after + down_bias_ref[...]
    grad_dense = jnp.zeros((tokens, width), F32)
    for index in range(chunks):
        pre = dot(dense_in, up_ref[index], 1, 0) + up_bias_ref[index]
        square = pre * pre
        bend = jnp.tanh(pre * (GELU_A + (GELU_A * GELU_B) * square))
        half = 0.5 + 0.5 * bend
        activated = (pre * half).astype(BF)
        slope = half + (pre * half) * (1.0 - bend) * (GELU_A + (3.0 * GELU_A * GELU_B) * square)
        result = result + dot(activated, down_ref[index], 1, 0)
        grad_pre = (slope * dot(low_stream, down_ref[index], 1, 1)).astype(BF)
        grad_dense = grad_dense + dot(grad_pre, up_ref[index], 1, 1)
        down_sum[index] += dot(activated, low_stream, 0, 0)
        up_sum[index] += dot(dense_in, grad_pre, 0, 0)
        hidden_grad[index] += jnp.sum(grad_pre.astype(F32), axis=0, keepdims=True)

    @pl.when(step >= 2)
    def _():
        drain(result_moves(step - 2, slot))
        drain(grad_moves(step - 2, slot))

    from_groups(result, result_box.at[slot], spare)
    begin(result_moves(step, slot))
    dense_rows, dense_gain_grad, dense_shift_grad = normalize_back(
        grad_dense, dense_gain_ref[...], dense_hat, dense_inverse
    )
    grad_after = stream + dense_rows

    low_grad = grad_after.astype(BF)
    output_sum[...] += dot(mixed_t[...], low_grad, 1, 0)
    low_mixed = dot(output_w[...], low_grad, 1, 1).astype(BF)
    delta = low_mixed.astype(F32) * mixed_t[...].astype(F32)
    delta = jnp.sum(delta.reshape(width // HEAD, HEAD, tokens), axis=1)
    for odd in (False, True):
        own = half_ones(odd, joined)
        key_extra = extra_columns(odd, joined, [key_first, key_second, ones, ones, ones])
        for pair in range(width // PAIR):
            head = 2 * pair + odd
            first = head * HEAD
            for part in range(tokens // joined):
                span = slice(part * joined, (part + 1) * joined)
                query_rows = query_t[first:first + HEAD, span]
                value_rows = value_t[first:first + HEAD, span]
                grad_rows = low_mixed[first:first + HEAD, span]
                keys = keys_s[span, pair * PAIR:(pair + 1) * PAIR]
                key_rows = keys.T[HEAD:] if odd else keys.T[:HEAD]
                high, middle, low = pieces(-logs[head:head + 1, span])
                right = stack_half(
                    odd, query_rows,
                    extra_rows(5, joined, [hide_first, hide_second, high, middle, low]),
                )
                high, middle, low = pieces(-delta[head:head + 1, span])
                value_right = jnp.concatenate(
                    [grad_rows, extra_rows(3, joined, [high, middle, low])], axis=0
                )
                value_left = jnp.concatenate(
                    [value_rows, extra_rows(3, joined, [one_row] * 3)], axis=0
                )
                shares = jnp.exp2(dot(keys * own + key_extra, right, 1, 0) * POWER)
                grad_shares = dot(value_left, value_right, 0, 0)
                low_scores = (shares * grad_shares).astype(BF)
                packed_grad[2 * width + first:2 * width + first + HEAD, span] = dot(
                    grad_rows, shares.astype(BF), 1, 1
                ).astype(BF)
                packed_grad[width + first:width + first + HEAD, span] = (
                    dot(query_rows, low_scores, 1, 1) * SCALE
                ).astype(BF)
                packed_grad[first:first + HEAD, span] = (
                    dot(key_rows, low_scores, 1, 0) * SCALE
                ).astype(BF)
    project_sum[...] += dot(packed_grad[...], normed, 1, 0)
    grad_normed = dot(packed_grad[...], project_t[...], 0, 0)
    grad_rows, gain_grad, shift_grad = normalize_back(grad_normed, gain_ref[...], hat, inverse)
    from_groups(grad_after + grad_rows, grad_box.at[slot], spare)
    begin(grad_moves(step, slot))
    vector_grad[0:1, :] += gain_grad
    vector_grad[1:2, :] += shift_grad
    vector_grad[2:3, :] += jnp.sum(low_grad.astype(F32), axis=0, keepdims=True)
    vector_grad[3:4, :] += dense_gain_grad
    vector_grad[4:5, :] += dense_shift_grad
    vector_grad[5:6, :] += jnp.sum(stream, axis=0, keepdims=True)

    @pl.when(step == pl.num_programs(0) - 1)
    def _():
        project_grad[...] = project_sum[...].T.astype(BF)
        output_grad[...] = output_sum[...].astype(BF)
        up_grad[...] = up_sum[...].astype(BF)
        down_grad[...] = down_sum[...].astype(BF)
        for send in cotangent_moves(step):
            send.wait_send()
        drain(result_moves(step, slot))
        drain(grad_moves(step, slot))
        if steps > 1:
            for send in cotangent_moves(step - 1):
                send.wait_send()
            drain(result_moves(step - 1, 1 - slot))
            drain(grad_moves(step - 1, 1 - slot))
        for hop in range(1, peers):
            source = (me + peers - hop) % peers
            arrived(results_ref.at[source], result_recvs.at[hop])
            arrived(grads_ref.at[source], grad_recvs.at[hop])


def whole(shape):
    return pl.BlockSpec(shape, lambda step: (0,) * len(shape), pipeline_mode=pl.Buffered(1))


def whole_out(shape):
    return pl.BlockSpec(shape, lambda step: (0,) * len(shape))


def call(kernel, grid, in_specs, out_specs, out_shape, scratch, name, flops, nbytes, remote=None):
    return pl.pallas_call(
        kernel,
        grid=(grid,),
        in_specs=in_specs,
        out_specs=out_specs,
        out_shape=[jax.ShapeDtypeStruct(*one) for one in out_shape],
        scratch_shapes=scratch,
        compiler_params=pltpu.CompilerParams(
            dimension_semantics=("arbitrary",), vmem_limit_bytes=LIMIT,
            collective_id=remote, has_side_effects=remote is not None,
        ),
        cost_estimate=pl.CostEstimate(flops=flops, bytes_accessed=nbytes, transcendentals=0),
        name=name,
    )


def split_project(project):
    width = project.shape[0]
    return (
        project[:, :width].T, project[:, width:2 * width], project[:, 2 * width:].T, project.T
    )


def body(
    peers,
    inputs, context, sample_mask,
    sample_gain, sample_shift, sample_project, sample_output, sample_bias,
    feature_gain, feature_shift, feature_project, feature_output, feature_bias,
    dense_gain, dense_shift, up_weight, up_bias, down_weight, down_bias,
    cotangent,
):
    _, local, samples, width = inputs.shape
    hidden = up_weight.shape[1]
    features = local * peers
    share = samples // peers
    group = 8
    chunk = 512
    chunks = hidden // chunk
    row = lambda vector: vector.reshape(1, -1)

    position = lax.iota(jnp.int32, samples)
    visible = (position < context[0]) & (sample_mask[0] == 1)
    mask = jnp.where(visible, 0.0, MASKED).astype(F32).reshape(samples, 1)
    query_w, key_w, value_w, project_t = split_project(sample_project)
    tokens = inputs[0]

    square = whole((width, width))
    line = whole((1, width))
    token_spec = pl.BlockSpec((1, samples, width), lambda step: (step, 0, 0))
    peer_spec = pl.BlockSpec((peers, 1, share, width), lambda step: (0, step, 0, 0))
    saved_spec = pl.BlockSpec((1, 3, samples, width), lambda step: (step, 0, 0, 0))
    log_spec = pl.BlockSpec((1, HEADS, samples), lambda step: (step, 0, 0))
    anywhere = pl.BlockSpec(memory_space=pl.ANY)
    peer_shape = (peers, local, share, width)
    sems = pltpu.SemaphoreType.DMA
    seen, saved, mixed, logs = call(
        functools.partial(sample_forward_kernel, peers), local,
        [token_spec, whole((samples, 1)), line, line, square, square, square, square, line],
        [anywhere, saved_spec, token_spec, log_spec],
        [
            (peer_shape, BF), ((local, 3, samples, width), BF),
            ((local, width, samples), BF), ((local, HEADS, samples), F32),
        ],
        [
            pltpu.VMEM((2, peers, share, width), BF), sems((2, peers)), sems((peers,)), sems((2,)),
        ],
        "sample_forward", 60_000_000_000, 30_000_000, 0,
    )(
        tokens, mask, row(sample_gain), row(sample_shift), query_w, key_w, value_w,
        sample_output, row(sample_bias),
    )

    query_f, key_f, value_f, project_ft = split_project(feature_project)
    block_tokens = features * group
    block_spec = pl.BlockSpec((features, group, width), lambda step: (0, step, 0))
    up_chunks = up_weight.reshape(width, chunks, chunk).transpose(1, 0, 2)
    down_chunks = down_weight.reshape(chunks, chunk, width)
    (
        result_returned, grad_returned, feature_project_grad, feature_output_grad, up_grad, down_grad,
        feature_vectors, hidden_grad,
    ) = call(
        functools.partial(feature_kernel, peers), share // group,
        [
            block_spec, anywhere, line, line, square, square, square, whole((3 * width, width)),
            square, line, line, line, whole((chunks, width, chunk)), whole((chunks, 1, chunk)),
            whole((chunks, chunk, width)), line,
        ],
        [
            anywhere, anywhere, whole_out((width, 3 * width)), whole_out((width, width)),
            whole_out((chunks, width, chunk)), whole_out((chunks, chunk, width)),
            whole_out((8, width)), whole_out((chunks, 1, chunk)),
        ],
        [
            (peer_shape, BF), (peer_shape, BF),
            ((width, 3 * width), BF), ((width, width), BF),
            ((chunks, width, chunk), BF), ((chunks, chunk, width), BF),
            ((8, width), F32), ((chunks, 1, chunk), F32),
        ],
        [
            pltpu.VMEM((3 * width, width), F32), pltpu.VMEM((width, width), F32),
            pltpu.VMEM((chunks, width, chunk), F32), pltpu.VMEM((chunks, chunk, width), F32),
            pltpu.VMEM((width // 128, block_tokens, 128), F32),
            pltpu.VMEM((width, block_tokens), BF),
            pltpu.VMEM((block_tokens, width), BF), pltpu.VMEM((width, block_tokens), BF),
            pltpu.VMEM((width, block_tokens), BF), pltpu.VMEM((HEADS, block_tokens), F32),
            pltpu.VMEM((3 * width, block_tokens), BF),
            pltpu.VMEM((share // group, features, group, width), BF),
            pltpu.VMEM((2, features, group, width), BF), pltpu.VMEM((2, features, group, width), BF),
            sems((2, peers)), sems((share // group,)), sems((2, peers)), sems((2, peers)),
            sems((peers,)), sems((peers,)), sems((2, 2)),
        ],
        "feature_block", 130_000_000_000, 40_000_000, 1,
    )(
        seen.reshape(features, share, width), cotangent[0],
        row(feature_gain), row(feature_shift), query_f, key_f, value_f, project_ft,
        feature_output, row(feature_bias), row(dense_gain), row(dense_shift),
        up_chunks, up_bias.reshape(chunks, 1, chunk), down_chunks, row(down_bias),
    )
    everyone = ("task", "feat")
    up_grad, down_grad, feature_project_grad, feature_output_grad = lax.psum(
        (up_grad, down_grad, feature_project_grad, feature_output_grad), everyone
    )
    (
        input_grad, output, sample_project_grad, sample_output_grad, sample_vectors,
    ) = call(
        sample_backward_kernel, local,
        [
            token_spec, whole((samples, 1)), line, line, whole((3 * width, width)), square,
            saved_spec, token_spec, log_spec, peer_spec, peer_spec,
        ],
        [
            token_spec, token_spec, whole_out((width, 3 * width)), whole_out((width, width)),
            whole_out((8, width)),
        ],
        [
            ((local, samples, width), F32), ((local, samples, width), BF),
            ((width, 3 * width), BF), ((width, width), BF), ((8, width), F32),
        ],
        [
            pltpu.VMEM((3 * width, width), F32), pltpu.VMEM((width, width), F32),
            pltpu.VMEM((3 * width, samples), BF),
        ],
        "sample_backward", 110_000_000_000, 50_000_000,
    )(
        tokens, mask, row(sample_gain), row(sample_shift), project_t, sample_output,
        saved, mixed, logs, grad_returned, result_returned,
    )
    vectors = jnp.concatenate(
        [sample_vectors, feature_vectors, hidden_grad.reshape(chunks, width)], axis=0
    )
    sample_project_grad, sample_output_grad = lax.psum(
        (sample_project_grad, sample_output_grad), everyone
    )
    vectors = lax.psum(vectors, everyone)
    wide = lambda array: array.astype(F32)
    return (
        output[None], input_grad[None],
        vectors[0], vectors[1], wide(sample_project_grad), wide(sample_output_grad), vectors[2],
        vectors[8], vectors[9], wide(feature_project_grad), wide(feature_output_grad), vectors[10],
        vectors[11], vectors[12],
        wide(up_grad).transpose(1, 0, 2).reshape(width, hidden), vectors[16:].reshape(hidden),
        wide(down_grad).reshape(hidden, width), vectors[13],
    )


def solution(mesh):
    split = P("task", "feat", None, None)
    return jax.shard_map(
        functools.partial(body, mesh.shape["feat"]),
        mesh=mesh,
        in_specs=(split, P("task"), P("task", None)) + (P(),) * 16 + (split,),
        out_specs=(split, split) + (P(),) * 16,
        check_vma=False,
    )
```

profile of v0, /device:TPU:0, one launch (start us, length us, event | category | flops | bytes accessed | tf_op | source)
XLA Modules:
  0.0 573.9 jit_solution(13921748013574944288)
XLA Ops:
  7.2 1.9 slice.49.key_w
  9.1 1.7 copy.45
  10.9 2.3 slice.52.key_w
  13.2 1.7 copy.48
  15.8 1.1 slice_bitcast_fusion.2
  16.9 1.0 slice_bitcast_fusion
  17.9 2.9 copy.51
  20.8 2.4 copy.52
  23.1 0.8 fusion.1.mask_ref
  23.9 59.0 %sample_forward.1 = (bf16[8,8,64,512]{3,2,1,0:T(8,128)(2,1)}, bf16[8,3,512,512]{3,2,1,0:T(8,128)(2,1)}, bf16[8,512,512]{2,1,0:T(8,128)(2,1)}, f32[8,8,512]{2,1,0:T(8,128)}) custom-call(bf16[8,512,512]{2,1,0:T(8,128)(2,1)} %bitcast.69, f32[512,1]{1,0:T(8,128)} %fusion.1.mask_ref, f32[1,512]{1,0:T(1,128)} %bitcast.80, f32[1,512]{1,0:T(1,128)} %bitcast.82, ...), custom_call_target="tpu_custom_call" | custom-call | flops 60000002048 | bytes 30000000 | tf_op jit(solution)/shard_map/sample_forward/pallas_call | solution.py:606
  82.9 212.4 %feature_block.1 = (bf16[8,8,64,512]{3,2,1,0:T(8,128)(2,1)}, bf16[8,8,64,512]{3,2,1,0:T(8,128)(2,1)}, bf16[512,1536]{1,0:T(8,128)(2,1)}, bf16[512,512]{1,0:T(8,1...) custom-call(bf16[64,64,512]{2,1,0:T(8,128)(2,1)} %bitcast.86, ...), custom_call_target="tpu_custom_call" | custom-call | flops 130000003072 | bytes 40000000 | tf_op jit(solution)/shard_map/feature_block/pallas_call | solution.py:631
  295.3 4.1 copy.53
  299.4 70.3 %sample_backward.1 = (f32[8,512,512]{2,1,0:T(8,128)}, bf16[8,512,512]{2,1,0:T(8,128)(2,1)}, bf16[512,1536]{1,0:T(8,128)(2,1)}, bf16[512,512]{1,0:T(8,128)(2,1)}, f32[8,512]{1,0:T(8,128)}) custom-call(bf16[8,512,512]{2,1,0:T(8,128)(2,1)} %bitcast.70, f32[512,1]{1,0:T(8,128)} %fusion.1.mask_ref, f32[1,512]{1,0:T(1,128)} %bitcast.81, f32[1,512]{1,0:T(1,128)} %bitcast.83, ...), custom_call_target="tpu_custom_call" | custom-call | flops 109999996928 | bytes 50000000 | tf_op jit(solution)/shard_map/sample_backward/pallas_call | solution.py:675
  369.8 0.6 copy-done.7
  370.5 42.0 %psum.49 = f32[20,512]{1,0:T(8,128)S(1)} all-reduce(f32[20,512]{1,0:T(8,128)S(1)} %pad_maximum_fusion), channel_id=1, replica_groups=mesh['task'=4,'feat'=8] {'task','feat'}, use_global_device_ids=true, to_apply=%region_0.1 | all-reduce | flops 10240 | bytes 81920 | tf_op jit(solution)/shard_map/psum | solution.py:704
  412.5 0.6 copy.56
  413.1 0.6 fusion.2
  413.7 137.5 %all-reduce.3.cloned.1.call-done = (bf16[512,2048]{0,1:T(8,128)(2,1)}, bf16[512,1536]{1,0:T(8,128)(2,1)}, bf16[512,512]{1,0:T(8,128)(2,1)}, bf16[512,1536]{1,0:T...) async-done(((bf16[512,2048]{0,1:T(8,128)(2,1)}, bf16[512,1536]{1,0:T(8,128)(2,1)}, bf16[512,512]{1,0:T(8,128)(2,1)}, bf16[512,1536]{1,0:T(8,128)(2,1)}, ...) | async-done | bytes 8388624 | tf_op jit(solution)/shard_map/psum | solution.py:670
  551.3 2.3 convert_element_type.15
  553.6 2.1 convert_element_type.17
  555.7 2.8 copy.54
  558.5 3.6 convert_element_type.14
  562.1 2.1 convert_element_type.16
  564.2 2.6 reshape.139
  (24 shorter events, 0.4 us)
Async XLA Ops:
  7.2 544.1 %all-reduce.3.cloned.1.call-start = ((), (), s32[]{:S(2)}) async-start(), calls=%async_computation | async-start | bytes 16777216 | tf_op jit(solution)/shard_map/psum | solution.py:670
  10.8 5.0 copy-start
  10.8 4.7 copy-start.8
  14.9 2.0 copy-start.1
  369.7 0.7 copy-start.7
  369.8 0.7 copy-start.5
  369.8 0.7 copy-start.6
  551.3 4.4 copy-start.3
  558.5 3.6 copy-start.4
  562.1 2.1 copy-start.2
Sparse Core Ops, SparseCore 0:
  369.9 181.2 all-reduce.2
where the time goes:
time: 583 us; the launch traced here: 574 us
  Pallas kernels  342 us (59%)
  waiting for transfers between devices  138 us (24%)
  blocking collectives  42 us (7%)
  local copies, waits for them, and re-layouts  24.1 us (4%)
  between operations  15 us (3%)
  other arithmetic  13.5 us (2%)
    pallas_call x1, Pallas kernels, body(): call(functools.partial(feature_kernel, peers), share // group, [block_spe...  212 us
    psum x1, waiting for transfers between devices, body(): lax.psum((up_grad, down_grad, feature_project_grad, feature_output_grad),...  138 us
    pallas_call x1, Pallas kernels, body(): call(sample_backward_kernel, local, [token_spec, whole((samples, 1)), lin...  70.3 us
    pallas_call x1, Pallas kernels, body(): call(functools.partial(sample_forward_kernel, peers), local, [token_spec,...  59 us
    psum x1, blocking collectives, body(): vectors = lax.psum(vectors, everyone)  42 us
  transfers between devices with their start and end apart: 1, of which 1 were waited for; matrix products, arithmetic and copies ran while one was open for 0% of the time, Pallas kernels for 0%

commit v1 on v0

--- a/solution.py
+++ b/solution.py
@@ -123,9 +123,9 @@
 
 def sample_forward_kernel(
     peers,
-    inputs_ref, mask_ref, gain_ref, shift_ref, query_w, key_w, value_w, output_w, bias_ref,
+    inputs_ref, mask_ref, gain_ref, shift_ref, project, output_w, bias_ref,
     seen_ref, saved_ref, mixed_ref, log_ref,
-    outbox, send_sems, recv_sems, own_sems,
+    turned, outbox, send_sems, recv_sems, own_sems,
 ):
     step = pl.program_id(0)
     steps = pl.num_programs(0)
@@ -135,6 +135,7 @@
     @pl.when(step == 0)
     def _():
         greet(peers, me)
+        turned[...] = project[...].T
 
     def moves(at, slot):
         sends = []
@@ -159,9 +160,9 @@
     samples, width = rows.shape
     hat, _ = normalize(rows)
     normed = (hat * gain_ref[...] + shift_ref[...]).astype(BF)
-    saved_ref[0, 0] = dot(query_w[...], normed, 1, 1).astype(BF)
-    saved_ref[0, 1] = dot(normed, key_w[...], 1, 0).astype(BF)
-    saved_ref[0, 2] = dot(value_w[...], normed, 1, 1).astype(BF)
+    saved_ref[0, 0] = dot(turned[:width], normed, 1, 1).astype(BF)
+    saved_ref[0, 1] = dot(normed, project[:, width:2 * width], 1, 0).astype(BF)
+    saved_ref[0, 2] = dot(turned[2 * width:], normed, 1, 1).astype(BF)
     mask = mask_ref[...]
     extra = extra_rows(1, samples, [jnp.ones((1, samples), F32)])
     for odd in (False, True):
@@ -200,15 +201,16 @@
 
 
 def sample_backward_kernel(
-    inputs_ref, mask_ref, gain_ref, shift_ref, project_t, output_w,
+    inputs_ref, mask_ref, gain_ref, shift_ref, project, output_w,
     saved_ref, mixed_ref, log_ref, grad_ref, result_ref,
-    input_grad_ref, final_ref, project_grad, output_grad, vector_grad,
-    project_sum, output_sum, packed_grad,
+    input_grad_ref, final_ref, project_grad, output_grad,
+    project_sum, output_sum, vector_grad, turned, packed_grad,
 ):
     step = pl.program_id(0)
 
     @pl.when(step == 0)
     def _():
+        turned[...] = project[...].T
         project_sum[...] = jnp.zeros_like(project_sum)
         output_sum[...] = jnp.zeros_like(output_sum)
         vector_grad[...] = jnp.zeros_like(vector_grad)
@@ -261,7 +263,7 @@
     hat, inverse = normalize(inputs_ref[0].astype(F32))
     normed = (hat * gain_ref[...] + shift_ref[...]).astype(BF)
     project_sum[...] += dot(packed_grad[...], normed, 1, 0)
-    grad_normed = dot(packed_grad[...], project_t[...], 0, 0)
+    grad_normed = dot(packed_grad[...], turned[...], 0, 0)
     grad_rows, grad_gain, grad_shift = normalize_back(grad_normed, gain_ref[...], hat, inverse)
     stream = low_grad.astype(F32)
     input_grad_ref[0] = stream + grad_rows
@@ -272,7 +274,8 @@
     @pl.when(step == pl.num_programs(0) - 1)
     def _():
         project_grad[...] = project_sum[...].T.astype(BF)
-        output_grad[...] = output_sum[...].astype(BF)
+        output_grad[:width] = output_sum[...].astype(BF)
+        output_grad[width:] = vector_grad[...].astype(BF)
 
 
 def to_groups(block_ref, spare):
@@ -303,10 +306,10 @@
 
 def feature_kernel(
     peers,
-    stream_ref, cotangent_hbm, gain_ref, shift_ref, query_w, key_w, value_w, project_t, output_w,
+    stream_ref, cotangent_hbm, gain_ref, shift_ref, project, output_w,
     bias_ref, dense_gain_ref, dense_shift_ref, up_ref, up_bias_ref, down_ref, down_bias_ref,
-    results_ref, grads_ref, project_grad, output_grad, up_grad, down_grad, vector_grad, hidden_grad,
-    project_sum, output_sum, up_sum, down_sum, spare, query_t, keys_s, value_t, mixed_t, logs,
+    results_ref, grads_ref, project_grad, output_grad, up_grad, down_grad,
+    vector_grad, hidden_grad, project_sum, output_sum, up_sum, down_sum, turned, spare, query_t, keys_s, value_t, mixed_t, logs,
     packed_grad, cotangents, result_box, grad_box,
     cotangent_sends, cotangent_recvs, result_sends, grad_sends, result_recvs, grad_recvs, own_sems,
 ):
@@ -316,7 +319,7 @@
     me = lax.axis_index("feat")
     local = features // peers
     share = steps * group
-    chunks, width, chunk = up_ref.shape
+    chunks, chunk, width = down_ref.shape
     tokens = features * group
     joined = 2 * features
 
@@ -380,6 +383,7 @@
     def _():
         greet(peers, me)
         start_cotangent(0)
+        turned[...] = project[...].T
 
     @pl.when(step + 1 < steps)
     def _():
@@ -402,9 +406,9 @@
     rows = to_groups(stream_ref, spare)
     hat, inverse = normalize(rows)
     normed = (hat * gain_ref[...] + shift_ref[...]).astype(BF)
-    query_t[...] = dot(query_w[...], normed, 1, 1).astype(BF)
-    keys_s[...] = dot(normed, key_w[...], 1, 0).astype(BF)
-    value_t[...] = dot(value_w[...], normed, 1, 1).astype(BF)
+    query_t[...] = dot(turned[:width], normed, 1, 1).astype(BF)
+    keys_s[...] = dot(normed, project[:, width:2 * width], 1, 0).astype(BF)
+    value_t[...] = dot(turned[2 * width:], normed, 1, 1).astype(BF)
     place = lax.broadcasted_iota(jnp.int32, (joined, 1), 0)
     place_row = lax.broadcasted_iota(jnp.int32, (1, joined), 1)
     key_first = (place < features).astype(F32)
@@ -439,7 +443,8 @@
     result = after + down_bias_ref[...]
     grad_dense = jnp.zeros((tokens, width), F32)
     for index in range(chunks):
-        pre = dot(dense_in, up_ref[index], 1, 0) + up_bias_ref[index]
+        up = up_ref[:, index * chunk:(index + 1) * chunk]
+        pre = dot(dense_in, up, 1, 0) + up_bias_ref[index]
         square = pre * pre
         bend = jnp.tanh(pre * (GELU_A + (GELU_A * GELU_B) * square))
         half = 0.5 + 0.5 * bend
@@ -447,7 +452,7 @@
         slope = half + (pre * half) * (1.0 - bend) * (GELU_A + (3.0 * GELU_A * GELU_B) * square)
         result = result + dot(activated, down_ref[index], 1, 0)
         grad_pre = (slope * dot(low_stream, down_ref[index], 1, 1)).astype(BF)
-        grad_dense = grad_dense + dot(grad_pre, up_ref[index], 1, 1)
+        grad_dense = grad_dense + dot(grad_pre, up, 1, 1)
         down_sum[index] += dot(activated, low_stream, 0, 0)
         up_sum[index] += dot(dense_in, grad_pre, 0, 0)
         hidden_grad[index] += jnp.sum(grad_pre.astype(F32), axis=0, keepdims=True)
@@ -507,7 +512,7 @@
                     dot(key_rows, low_scores, 1, 0) * SCALE
                 ).astype(BF)
     project_sum[...] += dot(packed_grad[...], normed, 1, 0)
-    grad_normed = dot(packed_grad[...], project_t[...], 0, 0)
+    grad_normed = dot(packed_grad[...], turned[...], 0, 0)
     grad_rows, gain_grad, shift_grad = normalize_back(grad_normed, gain_ref[...], hat, inverse)
     from_groups(grad_after + grad_rows, grad_box.at[slot], spare)
     begin(grad_moves(step, slot))
@@ -521,8 +526,14 @@
     @pl.when(step == pl.num_programs(0) - 1)
     def _():
         project_grad[...] = project_sum[...].T.astype(BF)
-        output_grad[...] = output_sum[...].astype(BF)
-        up_grad[...] = up_sum[...].astype(BF)
+        output_grad[:width] = output_sum[...].astype(BF)
+        output_grad[width:] = jnp.concatenate(
+            [vector_grad[...]]
+            + [hidden_grad[index].reshape(chunk // width, width) for index in range(chunks)]
+            + [jnp.zeros((8 - hidden_grad.size // width, width), F32)], axis=0,
+        ).astype(BF)
+        for index in range(chunks):
+            up_grad[:, index * chunk:(index + 1) * chunk] = up_sum[index].astype(BF)
         down_grad[...] = down_sum[...].astype(BF)
         for send in cotangent_moves(step):
             send.wait_send()
@@ -561,13 +572,6 @@
         ),
         cost_estimate=pl.CostEstimate(flops=flops, bytes_accessed=nbytes, transcendentals=0),
         name=name,
-    )
-
-
-def split_project(project):
-    width = project.shape[0]
-    return (
-        project[:, :width].T, project[:, width:2 * width], project[:, 2 * width:].T, project.T
     )
 
 
@@ -591,7 +595,6 @@
     position = lax.iota(jnp.int32, samples)
     visible = (position < context[0]) & (sample_mask[0] == 1)
     mask = jnp.where(visible, 0.0, MASKED).astype(F32).reshape(samples, 1)
-    query_w, key_w, value_w, project_t = split_project(sample_project)
     tokens = inputs[0]
 
     square = whole((width, width))
@@ -605,51 +608,47 @@
     sems = pltpu.SemaphoreType.DMA
     seen, saved, mixed, logs = call(
         functools.partial(sample_forward_kernel, peers), local,
-        [token_spec, whole((samples, 1)), line, line, square, square, square, square, line],
+        [token_spec, whole((samples, 1)), line, line, whole((width, 3 * width)), square, line],
         [anywhere, saved_spec, token_spec, log_spec],
         [
             (peer_shape, BF), ((local, 3, samples, width), BF),
             ((local, width, samples), BF), ((local, HEADS, samples), F32),
         ],
         [
-            pltpu.VMEM((2, peers, share, width), BF), sems((2, peers)), sems((peers,)), sems((2,)),
+            pltpu.VMEM((3 * width, width), BF), pltpu.VMEM((2, peers, share, width), BF),
+            sems((2, peers)), sems((peers,)), sems((2,)),
         ],
         "sample_forward", 60_000_000_000, 30_000_000, 0,
     )(
-        tokens, mask, row(sample_gain), row(sample_shift), query_w, key_w, value_w,
-        sample_output, row(sample_bias),
-    )
-
-    query_f, key_f, value_f, project_ft = split_project(feature_project)
+        tokens, mask, row(sample_gain), row(sample_shift), sample_project, sample_output, row(sample_bias),
+    )
+
     block_tokens = features * group
     block_spec = pl.BlockSpec((features, group, width), lambda step: (0, step, 0))
-    up_chunks = up_weight.reshape(width, chunks, chunk).transpose(1, 0, 2)
     down_chunks = down_weight.reshape(chunks, chunk, width)
     (
         result_returned, grad_returned, feature_project_grad, feature_output_grad, up_grad, down_grad,
-        feature_vectors, hidden_grad,
     ) = call(
         functools.partial(feature_kernel, peers), share // group,
         [
-            block_spec, anywhere, line, line, square, square, square, whole((3 * width, width)),
-            square, line, line, line, whole((chunks, width, chunk)), whole((chunks, 1, chunk)),
+            block_spec, anywhere, line, line, whole((width, 3 * width)),
+            square, line, line, line, whole((width, hidden)), whole((chunks, 1, chunk)),
             whole((chunks, chunk, width)), line,
         ],
         [
-            anywhere, anywhere, whole_out((width, 3 * width)), whole_out((width, width)),
-            whole_out((chunks, width, chunk)), whole_out((chunks, chunk, width)),
-            whole_out((8, width)), whole_out((chunks, 1, chunk)),
+            anywhere, anywhere, whole_out((width, 3 * width)), whole_out((width + 16, width)),
+            whole_out((width, hidden)), whole_out((chunks, chunk, width)),
         ],
         [
             (peer_shape, BF), (peer_shape, BF),
-            ((width, 3 * width), BF), ((width, width), BF),
-            ((chunks, width, chunk), BF), ((chunks, chunk, width), BF),
-            ((8, width), F32), ((chunks, 1, chunk), F32),
-        ],
-        [
+            ((width, 3 * width), BF), ((width + 16, width), BF),
+            ((width, hidden), BF), ((chunks, chunk, width), BF),
+        ],
+        [
+            pltpu.VMEM((8, width), F32), pltpu.VMEM((chunks, 1, chunk), F32),
             pltpu.VMEM((3 * width, width), F32), pltpu.VMEM((width, width), F32),
             pltpu.VMEM((chunks, width, chunk), F32), pltpu.VMEM((chunks, chunk, width), F32),
-            pltpu.VMEM((width // 128, block_tokens, 128), F32),
+            pltpu.VMEM((3 * width, width), BF), pltpu.VMEM((width // 128, block_tokens, 128), F32),
             pltpu.VMEM((width, block_tokens), BF),
             pltpu.VMEM((block_tokens, width), BF), pltpu.VMEM((width, block_tokens), BF),
             pltpu.VMEM((width, block_tokens), BF), pltpu.VMEM((HEADS, block_tokens), F32),
@@ -662,54 +661,54 @@
         "feature_block", 130_000_000_000, 40_000_000, 1,
     )(
         seen.reshape(features, share, width), cotangent[0],
-        row(feature_gain), row(feature_shift), query_f, key_f, value_f, project_ft,
+        row(feature_gain), row(feature_shift), feature_project,
         feature_output, row(feature_bias), row(dense_gain), row(dense_shift),
-        up_chunks, up_bias.reshape(chunks, 1, chunk), down_chunks, row(down_bias),
+        up_weight, up_bias.reshape(chunks, 1, chunk), down_chunks, row(down_bias),
     )
     everyone = ("task", "feat")
-    up_grad, down_grad, feature_project_grad, feature_output_grad = lax.psum(
+    feature_grads = lax.psum(
         (up_grad, down_grad, feature_project_grad, feature_output_grad), everyone
     )
     (
-        input_grad, output, sample_project_grad, sample_output_grad, sample_vectors,
+        input_grad, output, sample_project_grad, sample_output_grad,
     ) = call(
         sample_backward_kernel, local,
         [
-            token_spec, whole((samples, 1)), line, line, whole((3 * width, width)), square,
+            token_spec, whole((samples, 1)), line, line, whole((width, 3 * width)), square,
             saved_spec, token_spec, log_spec, peer_spec, peer_spec,
         ],
         [
-            token_spec, token_spec, whole_out((width, 3 * width)), whole_out((width, width)),
-            whole_out((8, width)),
+            token_spec, token_spec, whole_out((width, 3 * width)), whole_out((width + 16, width)),
         ],
         [
             ((local, samples, width), F32), ((local, samples, width), BF),
-            ((width, 3 * width), BF), ((width, width), BF), ((8, width), F32),
+            ((width, 3 * width), BF), ((width + 16, width), BF),
         ],
         [
             pltpu.VMEM((3 * width, width), F32), pltpu.VMEM((width, width), F32),
-            pltpu.VMEM((3 * width, samples), BF),
+            pltpu.VMEM((16, width), F32),
+            pltpu.VMEM((3 * width, width), BF), pltpu.VMEM((3 * width, samples), BF),
         ],
         "sample_backward", 110_000_000_000, 50_000_000,
     )(
-        tokens, mask, row(sample_gain), row(sample_shift), project_t, sample_output,
+        tokens, mask, row(sample_gain), row(sample_shift), sample_project, sample_output,
         saved, mixed, logs, grad_returned, result_returned,
     )
-    vectors = jnp.concatenate(
-        [sample_vectors, feature_vectors, hidden_grad.reshape(chunks, width)], axis=0
-    )
-    sample_project_grad, sample_output_grad = lax.psum(
-        (sample_project_grad, sample_output_grad), everyone
-    )
-    vectors = lax.psum(vectors, everyone)
+    sample_grads, feature_grads = lax.optimization_barrier(
+        ((sample_project_grad, sample_output_grad), feature_grads)
+    )
+    sample_project_grad, sample_output_grad = lax.psum(sample_grads, everyone)
+    up_grad, down_grad, feature_project_grad, feature_output_grad = feature_grads
     wide = lambda array: array.astype(F32)
+    sample_vectors = wide(sample_output_grad[width:])
+    feature_vectors = wide(feature_output_grad[width:])
     return (
         output[None], input_grad[None],
-        vectors[0], vectors[1], wide(sample_project_grad), wide(sample_output_grad), vectors[2],
-        vectors[8], vectors[9], wide(feature_project_grad), wide(feature_output_grad), vectors[10],
-        vectors[11], vectors[12],
-        wide(up_grad).transpose(1, 0, 2).reshape(width, hidden), vectors[16:].reshape(hidden),
-        wide(down_grad).reshape(hidden, width), vectors[13],
+        sample_vectors[0], sample_vectors[1], wide(sample_project_grad), wide(sample_output_grad[:width]),
+        sample_vectors[2], feature_vectors[0], feature_vectors[1], wide(feature_project_grad),
+        wide(feature_output_grad[:width]), feature_vectors[2], feature_vectors[3], feature_vectors[4],
+        wide(up_grad), feature_vectors[8:8 + hidden // width].reshape(hidden), wide(down_grad).reshape(hidden, width),
+        feature_vectors[5],
     )
 
 

time: 583 us -> 588 us (level); the launches traced: 574 us -> 587 us
  waiting for transfers between devices: 138 us -> 218 us
  blocking collectives: 42 us -> 0 us
  local copies, waits for them, and re-layouts: 24.1 us -> 2.01 us
  Pallas kernels: 342 us -> 334 us
    psum x0 -> x1, waiting for transfers between devices: none -> 130 us  [body(): sample_project_grad, sample_output_grad = lax.psum(sample_grads, everyone)]
    psum x1, waiting for transfers between devices: 138 us -> 87.5 us  [body(): lax.psum((up_grad, down_grad, feature_project_grad, feature_output_grad),...]
    psum x1 -> x0, blocking collectives: 42 us -> none  [body(): vectors = lax.psum(vectors, everyone)]
    unnamed x25 -> x8, local copies, waits for them, and re-layouts: 10.5 us -> 0.62 us
    pallas_call x1, Pallas kernels: 212 us -> 204 us  [body(): call(functools.partial(feature_kernel, peers), share // group, [block_spe...]
    transpose x3 -> x0, local copies, waits for them, and re-layouts: 6.25 us -> none  [the longest x1 4.14 us: body(): wide(up_grad).transpose(1, 0, 2).reshape(width, hidden)]
    convert_element_type x4 -> x7, other arithmetic: 10.1 us -> 14.3 us  [body(): wide = lambda array: array.astype(F32)]
  transfers between devices with their start and end apart: 1 -> 2, of which waited for: 1 -> 2; matrix products, arithmetic and copies ran while one was open for 0% -> 1% of each run, Pallas kernels for 0% -> 12%
where the time goes in v1:
time: 588 us; the launch traced here: 587 us
  Pallas kernels  334 us (57%)
  waiting for transfers between devices  218 us (37%)
  other arithmetic  18.5 us (3%)
  between operations  14.7 us (2%)
    pallas_call x1, Pallas kernels, body(): call(functools.partial(feature_kernel, peers), share // group, [block_spe...  204 us
    psum x1, waiting for transfers between devices, body(): sample_project_grad, sample_output_grad = lax.psum(sample_grads, everyone)  130 us
    psum x1, waiting for transfers between devices, body(): lax.psum((up_grad, down_grad, feature_project_grad, feature_output_grad),...  87.5 us
    pallas_call x1, Pallas kernels, body(): call(sample_backward_kernel, local, [token_spec, whole((samples, 1)), lin...  70.8 us
    pallas_call x1, Pallas kernels, body(): call(functools.partial(sample_forward_kernel, peers), local, [token_spec,...  59.4 us
    convert_element_type x7, other arithmetic, body(): wide = lambda array: array.astype(F32)  14.3 us
  transfers between devices with their start and end apart: 2, of which 2 were waited for; matrix products, arithmetic and copies ran while one was open for 1% of the time, Pallas kernels for 12%

profile of v1, /device:TPU:0, one launch (start us, length us, event | category | flops | bytes accessed | tf_op | source)
XLA Modules:
  0.0 587.5 jit_solution(9874526432801659273)
XLA Ops:
  7.2 0.0 all-reduce.7.cloned.1.call-start
  7.9 0.7 compare_bitcast_fusion
  8.6 0.2 copy.38
  8.8 0.8 fusion.1.mask_ref
  9.5 59.4 %sample_forward.1 = (bf16[8,8,64,512]{3,2,1,0:T(8,128)(2,1)}, bf16[8,3,512,512]{3,2,1,0:T(8,128)(2,1)}, bf16[8,512,512]{2,1,0:T(8,128)(2,1)}, f32[8,8,512]{2,1,0:T(8,128)}) custom-call(bf16[8,512,512]{2,1,0:T(8,128)(2,1)} %bitcast.46, f32[512,1]{1,0:T(8,128)} %fusion.1.mask_ref, f32[1,512]{1,0:T(1,128)} %bitcast.57, f32[1,512]{1,0:T(1,128)} %bitcast.59, ...), custom_call_target="tpu_custom_call" | custom-call | flops 60000002048 | bytes 30000000 | tf_op jit(solution)/shard_map/sample_forward/pallas_call | solution.py:609
  69.0 204.2 %feature_block.1 = (bf16[8,8,64,512]{3,2,1,0:T(8,128)(2,1)}, bf16[8,8,64,512]{3,2,1,0:T(8,128)(2,1)}, bf16[512,1536]{1,0:T(8,128)(2,1)}, bf16[528,512]{1,0:T(8,1...) custom-call(bf16[64,64,512]{2,1,0:T(8,128)(2,1)} %bitcast.63, bf16[8,512,512]{2,1,0:T(8,128)(2,1)} %bitcast.45, ...), custom_call_target="tpu_custom_call" | custom-call | flops 130000003072 | bytes 40000000 | tf_op jit(solution)/shard_map/feature_block/pallas_call | solution.py:631
  273.2 0.0 all-reduce.7.cloned.1.call-update
  273.2 0.0 all-reduce.5.cloned.1.call-start
  273.2 70.8 %sample_backward.1 = (f32[8,512,512]{2,1,0:T(8,128)}, bf16[8,512,512]{2,1,0:T(8,128)(2,1)}, bf16[512,1536]{1,0:T(8,128)(2,1)}, bf16[528,512]{1,0:T(8,128)(2,1)}) custom-call(bf16[8,512,512]{2,1,0:T(8,128)(2,1)} %bitcast.47, f32[512,1]{1,0:T(8,128)} %fusion.1.mask_ref, f32[1,512]{1,0:T(1,128)} %bitcast.58, f32[1,512]{1,0:T(1,128)} %bitcast.60, ...), custom_call_target="tpu_custom_call" | custom-call | flops 109999996928 | bytes 50000000 | tf_op jit(solution)/shard_map/sample_backward/pallas_call | solution.py:674
  344.0 87.5 %all-reduce.7.cloned.1.call-done = (bf16[512,2048]{1,0:T(8,128)(2,1)}, bf16[4,512,512]{2,1,0:T(8,128)(2,1)}, bf16[512,1536]{1,0:T(8,128)(2,1)}, bf16[528,512]{1,0:T(8,128)(2,1)}) async-done(((bf16[512,2048]{1,0:T(8,128)(2,1)}, bf16[4,512,512]{2,1,0:T(8,128)(2,1)}, bf16[512,1536]{1,0:T(8,128)(2,1)}, bf16[528,512]{1,0:T(8,128)(2,1)}), (bf16[512,2048]{1,0:T(8,128)(2,1)}, bf16[4,512,512]{2,1,0:T(8,128)(2,1)}, ...) | async-done | bytes 6307856 | tf_op jit(solution)/shard_map/psum | solution.py:669
  431.5 0.9 slice_convert_fusion.3
  432.4 0.6 copy.39
  433.0 3.5 convert_element_type.26
  436.5 0.0 copy-done.1
  436.5 2.5 convert_element_type.28
  439.0 0.0 all-reduce.5.cloned.1.call-update
  439.0 0.6 fusion.2
  439.6 1.1 slice_convert_fusion.1
  440.8 2.7 bitcast_convert_fusion
  443.5 130.2 %all-reduce.5.cloned.1.call-done = (bf16[528,512]{1,0:T(8,128)(2,1)}, bf16[512,1536]{1,0:T(8,128)(2,1)}) async-done(((bf16[528,512]{1,0:T(8,128)(2,1)}, bf16[512,1536]{1,0:T(8,128)(2,1)}), (bf16[528,512]{1,0:T(8,128)(2,1)}, bf16[512,1536]{1,0:T(8,128)(2,1)})) %all-reduce.5.cloned.1.call-update) | async-done | bytes 2113552 | tf_op jit(solution)/shard_map/psum | solution.py:700
  573.7 0.7 slice_convert_fusion.2
  574.4 2.1 slice_convert_fusion
  576.6 0.6 fusion.3
  577.2 3.5 convert_element_type.23
  (6 shorter events, 0.0 us)
Async XLA Ops:
  7.2 424.3 %all-reduce.7.cloned.1.call-start = ((), (), s32[]{:S(2)}) async-start(), calls=%async_computation.1 | async-start | bytes 12615680 | tf_op jit(solution)/shard_map/psum | solution.py:669
  273.2 300.5 %all-reduce.5.cloned.1.call-start = ((), (), s32[]{:S(2)}) async-start(), calls=%async_computation | async-start | bytes 4227072 | tf_op jit(solution)/shard_map/psum | solution.py:700
  431.5 5.0 copy-start.1
  436.5 3.2 copy-start.2
  439.0 1.7 copy-start
Sparse Core Ops, SparseCore 0:
  273.3 158.1 all-reduce.6
  439.2 134.4 all-reduce.4

commit v2 on v1

--- a/solution.py
+++ b/solution.py
@@ -21,6 +21,9 @@
 F32 = jnp.float32
 LIMIT = 60 * 1024 * 1024
 MESH = pl.DeviceIdType.MESH
+TILE = 16
+LANES = 128
+TICKS = 4
 
 
 def dot(left, right, left_dim, right_dim):
@@ -200,23 +203,131 @@
             arrived(seen_ref.at[(me + peers - hop) % peers], recv_sems.at[hop])
 
 
+def axis_orders(peers, tasks):
+    feat_bits = peers.bit_length() - 1
+    split = 1 + (feat_bits - 1) // 2
+    core = [("feat", 0)]
+    across = [("feat", bit) for bit in range(1, split)]
+    along = [("feat", bit) for bit in range(split, feat_bits)]
+    task = [("task", bit) for bit in range(tasks.bit_length() - 1)]
+    return core + across + along + task, core + along + across + task
+
+
 def sample_backward_kernel(
+    peers, tasks, feature_jobs, sample_jobs,
     inputs_ref, mask_ref, gain_ref, shift_ref, project, output_w,
-    saved_ref, mixed_ref, log_ref, grad_ref, result_ref,
-    input_grad_ref, final_ref, project_grad, output_grad,
+    saved_ref, mixed_ref, log_ref, grad_ref, feature_vectors, feature_stacked,
+    input_grad_ref, summed_ref, vectors_ref,
     project_sum, output_sum, vector_grad, turned, packed_grad,
+    parts, inbox, full, vector_parts, vector_inbox,
+    load_sems, store_sems, sends, recvs, vector_sends, vector_recvs,
 ):
     step = pl.program_id(0)
+    steps = pl.num_programs(0)
+    orders = axis_orders(peers, tasks)
+    bits = len(orders[0])
+    size = parts.shape[2]
+    place = {"feat": lax.axis_index("feat"), "task": lax.axis_index("task")}
+
+    def side(axis, bit):
+        return (place[axis] // 2 ** bit) % 2
+
+    def partner(axis, bit):
+        return {axis: place[axis] + (1 - 2 * side(axis, bit)) * 2 ** bit}
+
+    bases = []
+    for order in orders:
+        base = [0]
+        for index, where in enumerate(order):
+            base.append(base[-1] + side(*where) * (size >> (index + 1)))
+        bases.append(base)
+
+    def exchange(job, lane, stage):
+        index = stage if stage < bits else 2 * bits - 1 - stage
+        where = orders[lane][index]
+        part = size >> (index + 1)
+        if stage < bits:
+            gone = bases[lane][index] + (1 - side(*where)) * part
+            source = parts.at[job, lane, pl.ds(gone, part)]
+            target = inbox.at[job, lane, pl.ds(size - (size >> index), part)]
+        else:
+            source = target = full.at[job, lane, pl.ds(bases[lane][index + 1], part)]
+        return pltpu.make_async_remote_copy(
+            src_ref=source, dst_ref=target, send_sem=sends.at[job % 2, lane, stage],
+            recv_sem=recvs.at[job % 2, lane, stage], device_id=partner(*where),
+            device_id_type=MESH,
+        )
+
+    def load(job):
+        return pltpu.make_async_copy(feature_stacked.at[job], parts.at[job], load_sems.at[job])
+
+    def store(job):
+        return pltpu.make_async_copy(full.at[job], summed_ref.at[job], store_sems.at[job])
+
+    def advance(action, job, loaded):
+        if action == 0 and loaded:
+            load(job).wait()
+        for lane in range(2):
+            if action > 0:
+                exchange(job, lane, action - 1).wait()
+            if 0 < action <= bits:
+                part = size >> action
+                kept = pl.ds(bases[lane][action], part)
+                arrival = inbox[job, lane, pl.ds(size - 2 * part, part)].astype(F32)
+                total = (parts[job, lane, kept].astype(F32) + arrival).astype(BF)
+                if action < bits:
+                    parts[job, lane, kept] = total
+                else:
+                    full[job, lane, kept] = total
+            if action < 2 * bits:
+                exchange(job, lane, action).start()
+        if action == 2 * bits:
+            store(job).start()
+
+    offsets = [3 * action // 2 for action in range(2 * bits + 1)]
+    first_sample = max(steps, feature_jobs)
+
+    def tick(point):
+        for action in reversed(range(2 * bits + 1)):
+            if offsets[action] % TICKS == point:
+                job = step - offsets[action] // TICKS
+
+                @pl.when((job >= 0) & (job < feature_jobs))
+                def _():
+                    advance(action, job, True)
+
+    def vector_exchange(stage):
+        return pltpu.make_async_remote_copy(
+            src_ref=vector_parts.at[stage], dst_ref=vector_inbox.at[stage],
+            send_sem=vector_sends.at[stage], recv_sem=vector_recvs.at[stage],
+            device_id=partner(*orders[0][stage]), device_id_type=MESH,
+        )
+
+    def vector_advance(action):
+        if action > 0:
+            vector_exchange(action - 1).wait()
+            vector_parts[action] = vector_parts[action - 1] + vector_inbox[action - 1]
+        if action < bits:
+            vector_exchange(action).start()
+        else:
+            vectors_ref[...] = vector_parts[bits]
 
     @pl.when(step == 0)
     def _():
+        barrier = pltpu.get_barrier_semaphore()
+        for where in orders[0]:
+            pl.semaphore_signal(
+                barrier, inc=1, device_id=partner(*where), device_id_type=MESH
+            )
+        for job in range(feature_jobs):
+            load(job).start()
         turned[...] = project[...].T
         project_sum[...] = jnp.zeros_like(project_sum)
         output_sum[...] = jnp.zeros_like(output_sum)
         vector_grad[...] = jnp.zeros_like(vector_grad)
+        pl.semaphore_wait(barrier, bits)
 
     samples, width = inputs_ref.shape[1:]
-    final_ref[0] = result_ref[...].reshape(samples, width)
     low_grad = grad_ref[...].reshape(samples, width)
     output_sum[...] += dot(mixed_ref[0], low_grad, 1, 0)
     grad_mixed = dot(output_w[...], low_grad, 1, 1)
@@ -233,6 +344,9 @@
         for pair in range(width // PAIR):
             head = 2 * pair + odd
             first = head * HEAD
+            done = odd * (width // PAIR) + pair
+            if done % (HEADS // TICKS) == 0:
+                tick(done // (HEADS // TICKS))
             lanes = slice(pair * PAIR, (pair + 1) * PAIR)
             query_rows = saved_ref[0, 0, first:first + HEAD, :]
             value_rows = saved_ref[0, 2, first:first + HEAD, :]
@@ -266,16 +380,71 @@
     grad_normed = dot(packed_grad[...], turned[...], 0, 0)
     grad_rows, grad_gain, grad_shift = normalize_back(grad_normed, gain_ref[...], hat, inverse)
     stream = low_grad.astype(F32)
-    input_grad_ref[0] = stream + grad_rows
+    input_grad_ref[0] = (stream + grad_rows).astype(BF)
     vector_grad[0:1, :] += grad_gain
     vector_grad[1:2, :] += grad_shift
     vector_grad[2:3, :] += jnp.sum(stream, axis=0, keepdims=True)
 
-    @pl.when(step == pl.num_programs(0) - 1)
+    @pl.when(step == steps - 1)
     def _():
-        project_grad[...] = project_sum[...].T.astype(BF)
-        output_grad[:width] = output_sum[...].astype(BF)
-        output_grad[width:] = vector_grad[...].astype(BF)
+        vector_parts[0] = jnp.concatenate([feature_vectors[...], vector_grad[...]], axis=0)
+        vector_advance(0)
+        sums = [project_sum.at[part * width:(part + 1) * width] for part in range(3)]
+        per_column = parts.shape[2] // 2
+        for piece, total in enumerate(sums + [output_sum]):
+            job, first = divmod(piece * width // TILE, per_column)
+            for column in range(width // LANES):
+                lane, inner = divmod(column, width // LANES // 2)
+                begin = inner * per_column + first
+                parts[feature_jobs + job, lane, begin:begin + width // TILE] = total[
+                    :, column * LANES:(column + 1) * LANES
+                ].astype(BF).reshape(width // TILE, TILE, LANES)
+        vector_at = 1
+        for at in range(steps, first_sample + sample_jobs + offsets[-1] // TICKS):
+            for point in range(TICKS):
+                for action in reversed(range(2 * bits + 1)):
+                    slot = at - offsets[action] // TICKS
+                    if offsets[action] % TICKS != point:
+                        continue
+                    if 0 <= slot < feature_jobs:
+                        advance(action, slot, True)
+                    if 0 <= slot - first_sample < sample_jobs:
+                        advance(action, feature_jobs + slot - first_sample, False)
+                if vector_at <= bits:
+                    vector_advance(vector_at)
+                    vector_at += 1
+        for late in range(vector_at, bits + 1):
+            vector_advance(late)
+        for job in range(feature_jobs + sample_jobs):
+            store(job).wait()
+
+
+def finish_kernel(
+    chunks, summed_ref, input_ref, result_ref,
+    up_grad, down_grad, feature_project, feature_output, sample_project, sample_output,
+    input_grad_ref, output_ref,
+):
+    step = pl.program_id(0)
+    _, rows, width = output_ref.shape
+    input_grad_ref[...] = input_ref[...].astype(F32)
+    output_ref[...] = result_ref[...].reshape(1, rows, width)
+    bounds = [
+        (up_grad, chunks, False), (down_grad, chunks, False), (feature_project, 3, True),
+        (feature_output, 1, False), (sample_project, 3, True), (sample_output, 1, False),
+    ]
+    start = 0
+    for target, count, turn in bounds:
+        @pl.when((step >= start) & (step < start + count))
+        def _():
+            for column in range(width // LANES):
+                piece = summed_ref[0, column].astype(F32)
+                span = slice(column * LANES, (column + 1) * LANES)
+                if turn:
+                    target[span, :] = piece.T
+                else:
+                    target[:, span] = piece
+
+        start += count
 
 
 def to_groups(block_ref, spare):
@@ -308,7 +477,7 @@
     peers,
     stream_ref, cotangent_hbm, gain_ref, shift_ref, project, output_w,
     bias_ref, dense_gain_ref, dense_shift_ref, up_ref, up_bias_ref, down_ref, down_bias_ref,
-    results_ref, grads_ref, project_grad, output_grad, up_grad, down_grad,
+    results_ref, grads_ref, stacked_ref, vectors_ref,
     vector_grad, hidden_grad, project_sum, output_sum, up_sum, down_sum, turned, spare, query_t, keys_s, value_t, mixed_t, logs,
     packed_grad, cotangents, result_box, grad_box,
     cotangent_sends, cotangent_recvs, result_sends, grad_sends, result_recvs, grad_recvs, own_sems,
@@ -525,16 +694,21 @@
 
     @pl.when(step == pl.num_programs(0) - 1)
     def _():
-        project_grad[...] = project_sum[...].T.astype(BF)
-        output_grad[:width] = output_sum[...].astype(BF)
-        output_grad[width:] = jnp.concatenate(
+        vectors_ref[...] = jnp.concatenate(
             [vector_grad[...]]
             + [hidden_grad[index].reshape(chunk // width, width) for index in range(chunks)]
             + [jnp.zeros((8 - hidden_grad.size // width, width), F32)], axis=0,
-        ).astype(BF)
-        for index in range(chunks):
-            up_grad[:, index * chunk:(index + 1) * chunk] = up_sum[index].astype(BF)
-        down_grad[...] = down_sum[...].astype(BF)
+        )
+        sums = [up_sum.at[index] for index in range(chunks)]
+        sums += [down_sum.at[index] for index in range(chunks)]
+        sums += [project_sum.at[part * width:(part + 1) * width] for part in range(3)]
+        rows_per_job = stacked_ref.shape[2]
+        for piece, total in enumerate(sums + [output_sum]):
+            job, first = divmod(piece * width, rows_per_job)
+            for column in range(width // LANES):
+                stacked_ref[job, column, first:first + width, :] = total[
+                    :, column * LANES:(column + 1) * LANES
+                ].astype(BF)
         for send in cotangent_moves(step):
             send.wait_send()
         drain(result_moves(step, slot))
@@ -576,7 +750,7 @@
 
 
 def body(
-    peers,
+    peers, tasks,
     inputs, context, sample_mask,
     sample_gain, sample_shift, sample_project, sample_output, sample_bias,
     feature_gain, feature_shift, feature_project, feature_output, feature_bias,
@@ -591,6 +765,13 @@
     chunk = 512
     chunks = hidden // chunk
     row = lambda vector: vector.reshape(1, -1)
+    columns = width // LANES
+    pieces_in = (2 * chunks + 4, 4)
+    size = max(LANES, peers * tasks)
+    job_rows = 2 * size * TILE // columns
+    feature_jobs, sample_jobs = (count * width // job_rows for count in pieces_in)
+    jobs = feature_jobs + sample_jobs
+    bits = (peers * tasks).bit_length() - 1
 
     position = lax.iota(jnp.int32, samples)
     visible = (position < context[0]) & (sample_mask[0] == 1)
@@ -626,9 +807,7 @@
     block_tokens = features * group
     block_spec = pl.BlockSpec((features, group, width), lambda step: (0, step, 0))
     down_chunks = down_weight.reshape(chunks, chunk, width)
-    (
-        result_returned, grad_returned, feature_project_grad, feature_output_grad, up_grad, down_grad,
-    ) = call(
+    result_returned, grad_returned, feature_stacked, feature_vectors = call(
         functools.partial(feature_kernel, peers), share // group,
         [
             block_spec, anywhere, line, line, whole((width, 3 * width)),
@@ -636,13 +815,12 @@
             whole((chunks, chunk, width)), line,
         ],
         [
-            anywhere, anywhere, whole_out((width, 3 * width)), whole_out((width + 16, width)),
-            whole_out((width, hidden)), whole_out((chunks, chunk, width)),
+            anywhere, anywhere, whole_out((feature_jobs, columns, job_rows, LANES)),
+            whole_out((16, width)),
         ],
         [
             (peer_shape, BF), (peer_shape, BF),
-            ((width, 3 * width), BF), ((width + 16, width), BF),
-            ((width, hidden), BF), ((chunks, chunk, width), BF),
+            ((feature_jobs, columns, job_rows, LANES), BF), ((16, width), F32),
         ],
         [
             pltpu.VMEM((8, width), F32), pltpu.VMEM((chunks, 1, chunk), F32),
@@ -665,57 +843,89 @@
         feature_output, row(feature_bias), row(dense_gain), row(dense_shift),
         up_weight, up_bias.reshape(chunks, 1, chunk), down_chunks, row(down_bias),
     )
-    everyone = ("task", "feat")
-    feature_grads = lax.psum(
-        (up_grad, down_grad, feature_project_grad, feature_output_grad), everyone
-    )
-    (
-        input_grad, output, sample_project_grad, sample_output_grad,
-    ) = call(
-        sample_backward_kernel, local,
+    stack_shape = (jobs, 2, size, TILE, LANES)
+    input_grad, summed, vectors = call(
+        functools.partial(sample_backward_kernel, peers, tasks, feature_jobs, sample_jobs), local,
         [
             token_spec, whole((samples, 1)), line, line, whole((width, 3 * width)), square,
-            saved_spec, token_spec, log_spec, peer_spec, peer_spec,
-        ],
-        [
-            token_spec, token_spec, whole_out((width, 3 * width)), whole_out((width + 16, width)),
-        ],
-        [
-            ((local, samples, width), F32), ((local, samples, width), BF),
-            ((width, 3 * width), BF), ((width + 16, width), BF),
-        ],
+            saved_spec, token_spec, log_spec, peer_spec, whole((16, width)), anywhere,
+        ],
+        [token_spec, anywhere, whole_out((24, width))],
+        [((local, samples, width), BF), (stack_shape, BF), ((24, width), F32)],
         [
             pltpu.VMEM((3 * width, width), F32), pltpu.VMEM((width, width), F32),
-            pltpu.VMEM((16, width), F32),
+            pltpu.VMEM((8, width), F32),
             pltpu.VMEM((3 * width, width), BF), pltpu.VMEM((3 * width, samples), BF),
-        ],
-        "sample_backward", 110_000_000_000, 50_000_000,
+            pltpu.VMEM(stack_shape, BF), pltpu.VMEM(stack_shape, BF), pltpu.VMEM(stack_shape, BF),
+            pltpu.VMEM((bits + 1, 24, width), F32), pltpu.VMEM((bits, 24, width), F32),
+            sems((feature_jobs,)), sems((jobs,)), sems((2, 2, 2 * bits)), sems((2, 2, 2 * bits)),
+            sems((bits,)), sems((bits,)),
+        ],
+        "sample_backward", 110_000_000_000, 50_000_000, 2,
     )(
         tokens, mask, row(sample_gain), row(sample_shift), sample_project, sample_output,
-        saved, mixed, logs, grad_returned, result_returned,
+        saved, mixed, logs, grad_returned, feature_vectors,
+        feature_stacked.reshape((feature_jobs,) + stack_shape[1:]),
     )
-    sample_grads, feature_grads = lax.optimization_barrier(
-        ((sample_project_grad, sample_output_grad), feature_grads)
+    blocks = sum(pieces_in)
+    per_job = job_rows // width
+    per_feature = blocks // local
+    rows = samples // per_feature
+    token_rows = pl.BlockSpec(
+        (1, rows, width), lambda step: (step // per_feature, step % per_feature, 0)
     )
-    sample_project_grad, sample_output_grad = lax.psum(sample_grads, everyone)
-    up_grad, down_grad, feature_project_grad, feature_output_grad = feature_grads
-    wide = lambda array: array.astype(F32)
-    sample_vectors = wide(sample_output_grad[width:])
-    feature_vectors = wide(feature_output_grad[width:])
+
+    def piece_out(shape, start, count, across):
+        def place(step):
+            at = jnp.clip(step - start, 0, count - 1)
+            return (0, at) if across else (at, 0)
+
+        return pl.BlockSpec(shape, place)
+
+    (
+        up_grad, down_grad, feature_project_grad, feature_output_grad,
+        sample_project_grad, sample_output_grad, input_grad, output,
+    ) = call(
+        functools.partial(finish_kernel, chunks), blocks,
+        [
+            pl.BlockSpec(
+                (1, columns, width, LANES), lambda step: (step // per_job, 0, step % per_job, 0)
+            ),
+            token_rows,
+            pl.BlockSpec(
+                (peers // per_feature, 1, share, width),
+                lambda step: (step % per_feature, step // per_feature, 0, 0),
+            ),
+        ],
+        [
+            piece_out((width, chunk), 0, chunks, True),
+            piece_out((chunk, width), chunks, chunks, False),
+            piece_out((width, width), 2 * chunks, 3, True),
+            piece_out((width, width), 2 * chunks + 3, 1, True),
+            piece_out((width, width), 2 * chunks + 4, 3, True),
+            piece_out((width, width), 2 * chunks + 7, 1, True),
+            token_rows, token_rows,
+        ],
+        [
+            ((width, hidden), F32), ((hidden, width), F32), ((width, 3 * width), F32),
+            ((width, width), F32), ((width, 3 * width), F32), ((width, width), F32),
+            ((local, samples, width), F32), ((local, samples, width), BF),
+        ],
+        [], "finish", 0, 46_000_000,
+    )(summed.reshape(jobs, columns, job_rows, LANES), input_grad, result_returned)
     return (
         output[None], input_grad[None],
-        sample_vectors[0], sample_vectors[1], wide(sample_project_grad), wide(sample_output_grad[:width]),
-        sample_vectors[2], feature_vectors[0], feature_vectors[1], wide(feature_project_grad),
-        wide(feature_output_grad[:width]), feature_vectors[2], feature_vectors[3], feature_vectors[4],
-        wide(up_grad), feature_vectors[8:8 + hidden // width].reshape(hidden), wide(down_grad).reshape(hidden, width),
-        feature_vectors[5],
+        vectors[16], vectors[17], sample_project_grad, sample_output_grad,
+        vectors[18], vectors[0], vectors[1], feature_project_grad,
+        feature_output_grad, vectors[2], vectors[3], vectors[4],
+        up_grad, vectors[8:8 + hidden // width].reshape(hidden), down_grad, vectors[5],
     )
 
 
 def solution(mesh):
     split = P("task", "feat", None, None)
     return jax.shard_map(
-        functools.partial(body, mesh.shape["feat"]),
+        functools.partial(body, mesh.shape["feat"], mesh.shape["task"]),
         mesh=mesh,
         in_specs=(split, P("task"), P("task", None)) + (P(),) * 16 + (split,),
         out_specs=(split, split) + (P(),) * 16,

time: 588 us -> 476 us (0.81)
  waiting for transfers between devices: 218 us -> 0 us
  Pallas kernels: 334 us -> 467 us
  other arithmetic: 18.5 us -> 1.46 us
  between operations: 14.7 us -> 1.54 us
    psum x2 -> x0, waiting for transfers between devices: 218 us -> none  [the longest x1 130 us: body(): sample_project_grad, sample_output_grad = lax.psum(sample_grads, everyone)]
    pallas_call x1 -> x2, Pallas kernels: 70.8 us -> 191 us  [the longest x1 170 us: body(): call(functools.partial(sample_backward_kernel, peers, tasks, feature_jobs...]
    convert_element_type x7 -> x0, other arithmetic: 14.3 us -> none  [body(): wide = lambda array: array.astype(F32)]
    pallas_call x1, Pallas kernels: 204 us -> 217 us  [body(): call(functools.partial(feature_kernel, peers), share // group, [block_spe...]
  transfers between devices with their start and end apart: 2 -> 0, of which waited for: 2 -> 0; matrix products, arithmetic and copies ran while one was open for 1% -> 0% of each run, Pallas kernels for 12% -> 0%
where the time goes in v2:
time: 476 us; the launch traced here: 473 us
  Pallas kernels  467 us (98%)
    pallas_call x1, Pallas kernels, body(): call(functools.partial(feature_kernel, peers), share // group, [block_spe...  217 us
    pallas_call x1, Pallas kernels, body(): call(functools.partial(sample_backward_kernel, peers, tasks, feature_jobs...  170 us
    pallas_call x1, Pallas kernels, body(): call(functools.partial(sample_forward_kernel, peers), local, [token_spec,...  59.4 us
    pallas_call x1, Pallas kernels, body(): call(functools.partial(finish_kernel, chunks), blocks, [pl.BlockSpec((1,...  21 us

profile of v2, /device:TPU:0, one launch (start us, length us, event | category | flops | bytes accessed | tf_op | source)
XLA Modules:
  0.0 473.4 jit_solution(17870883110348316787)
XLA Ops:
  1.3 0.7 compare_bitcast_fusion
  2.0 0.2 copy.38
  2.2 0.8 fusion.1.mask_ref
  3.0 59.4 %sample_forward.1 = (bf16[8,8,64,512]{3,2,1,0:T(8,128)(2,1)}, bf16[8,3,512,512]{3,2,1,0:T(8,128)(2,1)}, bf16[8,512,512]{2,1,0:T(8,128)(2,1)}, f32[8,8,512]{2,1,0:T(8,128)}) custom-call(bf16[8,512,512]{2,1,0:T(8,128)(2,1)} %bitcast.47, f32[512,1]{1,0:T(8,128)} %fusion.1.mask_ref, f32[1,512]{1,0:T(1,128)} %bitcast.59, f32[1,512]{1,0:T(1,128)} %bitcast.61, ...), custom_call_target="tpu_custom_call" | custom-call | flops 60000002048 | bytes 30000000 | tf_op jit(solution)/shard_map/sample_forward/pallas_call | solution.py:790
  62.4 217.2 %feature_block.1 = (bf16[8,8,64,512]{3,2,1,0:T(8,128)(2,1)}, bf16[8,8,64,512]{3,2,1,0:T(8,128)(2,1)}, bf16[6,4,1024,128]{3,2,1,0:T(8,128)(2,1)}, f32[16,512]{1,0:T(8,128)}) custom-call(bf16[64,64,512]{2,1,0:T(8,128)(2,1)} %bitcast.64, bf16[8,512,512]{2,1,0:T(8,128)(2,1)} %bitcast.46, f32[1,512]{1,0:T(1,128)} %bitcast.53, f32[1,512]{1,0:T(1,128)} %bitcast.54, ...), custom_call_target="tpu_custom_call" | custom-call | flops 130000003072 | bytes 40000000 | tf_op jit(solution)/shard_map/feature_block/pallas_call | solution.py:810
  279.6 169.7 %sample_backward.1 = (bf16[8,512,512]{2,1,0:T(8,128)(2,1)}, bf16[8,2,128,16,128]{4,3,2,1,0:T(8,128)(2,1)}, f32[24,512]{1,0:T(8,128)}) custom-call(bf16[8,512,512]{2,1,0:T(8,128)(2,1)} %bitcast.48, f32[512,1]{1,0:T(8,128)} %fusion.1.mask_ref, f32[1,512]{1,0:T(1,128)} %bitcast.60, f32[1,512]{1,0:T(1,128)} %bitcast.62, bf16[512,1536]{1,0:T(8,128)(2,1)} %project.5, ...), custom_call_target="tpu_custom_call" | custom-call | flops 109999996928 | bytes 50000000 | tf_op jit(solution)/shard_map/sample_backward/pallas_call | solution.py:847
  449.3 0.7 slice_bitcast_fusion
  450.0 1.6 fusion.2
  451.6 0.6 copy.39
  452.2 21.0 %finish.1 = (f32[512,2048]{1,0:T(8,128)}, f32[2048,512]{1,0:T(8,128)}, f32[512,1536]{1,0:T(8,128)}, f32[512,512]{1,0:T(8,128)}, f32[512,1536]{1,0:T(8,128)}, /*i...) custom-call(bf16[8,4,1024,128]{3,2,1,0:T(8,128)(2,1)} %bitcast.34, ...), custom_call_target="tpu_custom_call" | custom-call | bytes 46000000 | tf_op jit(solution)/shard_map/finish/pallas_call | solution.py:888

commit v3 on v2

--- a/solution.py
+++ b/solution.py
@@ -23,7 +23,7 @@
 MESH = pl.DeviceIdType.MESH
 TILE = 16
 LANES = 128
-TICKS = 4
+TICKS = 2
 
 
 def dot(left, right, left_dim, right_dim):
@@ -205,12 +205,24 @@
 
 def axis_orders(peers, tasks):
     feat_bits = peers.bit_length() - 1
-    split = 1 + (feat_bits - 1) // 2
-    core = [("feat", 0)]
-    across = [("feat", bit) for bit in range(1, split)]
-    along = [("feat", bit) for bit in range(split, feat_bits)]
-    task = [("task", bit) for bit in range(tasks.bit_length() - 1)]
-    return core + across + along + task, core + along + across + task
+    task_bits = tasks.bit_length() - 1
+    half = (feat_bits - 1) // 2
+    core = ("feat", 0, 1)
+    across = ("feat", 1, half)
+    along = ("feat", 1 + half, feat_bits - 1 - half)
+    task = ("task", 0, task_bits)
+    kept = lambda order: [where for where in order if where[2] > 0]
+    return (
+        kept([core, across, along, task]), kept([core, along, across, task]),
+        kept([("feat", 0, feat_bits), task]),
+    )
+
+
+def hop_offsets(order):
+    offsets = [0]
+    for _, _, bits in order:
+        offsets.append(offsets[-1] + 2 ** bits - 1)
+    return offsets
 
 
 def sample_backward_kernel(
@@ -218,45 +230,60 @@
     inputs_ref, mask_ref, gain_ref, shift_ref, project, output_w,
     saved_ref, mixed_ref, log_ref, grad_ref, feature_vectors, feature_stacked,
     input_grad_ref, summed_ref, vectors_ref,
-    project_sum, output_sum, vector_grad, turned, packed_grad,
-    parts, inbox, full, vector_parts, vector_inbox,
+    project_sum, output_sum, vector_grad, turned, packed_all,
+    parts, inbox, full, feature_parts, feature_inbox, sample_parts, sample_inbox,
     load_sems, store_sems, sends, recvs, vector_sends, vector_recvs,
 ):
     step = pl.program_id(0)
     steps = pl.num_programs(0)
-    orders = axis_orders(peers, tasks)
-    bits = len(orders[0])
+    local = packed_all.shape[0]
+    *orders, vector_order = axis_orders(peers, tasks)
+    stages = len(orders[0])
+    last = 2 * stages
     size = parts.shape[2]
     place = {"feat": lax.axis_index("feat"), "task": lax.axis_index("task")}
 
-    def side(axis, bit):
-        return (place[axis] // 2 ** bit) % 2
-
-    def partner(axis, bit):
-        return {axis: place[axis] + (1 - 2 * side(axis, bit)) * 2 ** bit}
-
-    bases = []
+    def digit(where):
+        axis, bit, bits = where
+        return (place[axis] // 2 ** bit) % 2 ** bits
+
+    def partner(where, hop):
+        axis, bit, bits = where
+        own = digit(where)
+        return {axis: place[axis] + ((own + hop) % 2 ** bits - own) * 2 ** bit}
+
+    hops, bases, sizes = [], [], []
     for order in orders:
-        base = [0]
-        for index, where in enumerate(order):
-            base.append(base[-1] + side(*where) * (size >> (index + 1)))
+        hops.append(hop_offsets(order + order[::-1]))
+        base, left = [0], [size]
+        for where in order:
+            left.append(left[-1] >> where[2])
+            base.append(base[-1] + digit(where) * left[-1])
         bases.append(base)
-
-    def exchange(job, lane, stage):
-        index = stage if stage < bits else 2 * bits - 1 - stage
+        sizes.append(left)
+
+    def exchanges(job, lane, stage):
+        index = stage if stage < stages else last - 1 - stage
         where = orders[lane][index]
-        part = size >> (index + 1)
-        if stage < bits:
-            gone = bases[lane][index] + (1 - side(*where)) * part
-            source = parts.at[job, lane, pl.ds(gone, part)]
-            target = inbox.at[job, lane, pl.ds(size - (size >> index), part)]
-        else:
-            source = target = full.at[job, lane, pl.ds(bases[lane][index + 1], part)]
-        return pltpu.make_async_remote_copy(
-            src_ref=source, dst_ref=target, send_sem=sends.at[job % 2, lane, stage],
-            recv_sem=recvs.at[job % 2, lane, stage], device_id=partner(*where),
-            device_id_type=MESH,
-        )
+        part = sizes[lane][index + 1]
+        copies = []
+        for hop in range(1, 2 ** where[2]):
+            if stage < stages:
+                gone = bases[lane][index] + ((digit(where) + hop) % 2 ** where[2]) * part
+                source = parts.at[job, lane, pl.ds(gone, part)]
+                begin = size - sizes[lane][index] + (hop - 1) * part
+                target = inbox.at[job, lane, pl.ds(begin, part)]
+            else:
+                source = target = full.at[job, lane, pl.ds(bases[lane][index + 1], part)]
+            at = hops[lane][stage] + hop - 1
+            copies.append(
+                pltpu.make_async_remote_copy(
+                    src_ref=source, dst_ref=target, send_sem=sends.at[job, lane, at],
+                    recv_sem=recvs.at[job, lane, at], device_id=partner(where, hop),
+                    device_id_type=MESH,
+                )
+            )
+        return copies
 
     def load(job):
         return pltpu.make_async_copy(feature_stacked.at[job], parts.at[job], load_sems.at[job])
@@ -269,64 +296,164 @@
             load(job).wait()
         for lane in range(2):
             if action > 0:
-                exchange(job, lane, action - 1).wait()
-            if 0 < action <= bits:
-                part = size >> action
+                for copy in exchanges(job, lane, action - 1):
+                    copy.wait()
+            if 0 < action <= stages:
+                part = sizes[lane][action]
                 kept = pl.ds(bases[lane][action], part)
-                arrival = inbox[job, lane, pl.ds(size - 2 * part, part)].astype(F32)
-                total = (parts[job, lane, kept].astype(F32) + arrival).astype(BF)
-                if action < bits:
-                    parts[job, lane, kept] = total
+                total = parts[job, lane, kept].astype(F32)
+                for hop in range(1, 2 ** orders[lane][action - 1][2]):
+                    begin = size - sizes[lane][action - 1] + (hop - 1) * part
+                    total = total + inbox[job, lane, pl.ds(begin, part)].astype(F32)
+                if action < stages:
+                    parts[job, lane, kept] = total.astype(BF)
                 else:
-                    full[job, lane, kept] = total
-            if action < 2 * bits:
-                exchange(job, lane, action).start()
-        if action == 2 * bits:
+                    full[job, lane, kept] = total.astype(BF)
+            if action < last:
+                for copy in exchanges(job, lane, action):
+                    copy.start()
+        if action == last:
             store(job).start()
 
-    offsets = [3 * action // 2 for action in range(2 * bits + 1)]
-    first_sample = max(steps, feature_jobs)
-
-    def tick(point):
-        for action in reversed(range(2 * bits + 1)):
-            if offsets[action] % TICKS == point:
-                job = step - offsets[action] // TICKS
-
-                @pl.when((job >= 0) & (job < feature_jobs))
-                def _():
-                    advance(action, job, True)
-
-    def vector_exchange(stage):
-        return pltpu.make_async_remote_copy(
-            src_ref=vector_parts.at[stage], dst_ref=vector_inbox.at[stage],
-            send_sem=vector_sends.at[stage], recv_sem=vector_recvs.at[stage],
-            device_id=partner(*orders[0][stage]), device_id_type=MESH,
-        )
-
-    def vector_advance(action):
+    offsets = [0, 1] + [2 * action - 1 for action in range(2, last)] + [2 * last - 2]
+
+    def feature_tick(point):
+        for action in reversed(range(last + 1)):
+            job = TICKS * step + point - offsets[action]
+
+            @pl.when((job >= 0) & (job < feature_jobs))
+            def _():
+                advance(action, job, True)
+
+    def sample_tick():
+        for action in reversed(range(last + 1)):
+            job = step - local - action
+
+            @pl.when((job >= 0) & (job < sample_jobs))
+            def _():
+                advance(action, feature_jobs + job, False)
+
+    vector_hops = hop_offsets(vector_order)
+
+    def vector_exchanges(kind, stage):
+        source, target = [(feature_parts, feature_inbox), (sample_parts, sample_inbox)][kind]
+        where = vector_order[stage]
+        slot = vector_hops[stage] + stage + digit(where)
+        copies = []
+        for hop in range(1, 2 ** where[2]):
+            at = vector_hops[stage] + hop - 1
+            copies.append(
+                pltpu.make_async_remote_copy(
+                    src_ref=source.at[stage], dst_ref=target.at[slot],
+                    send_sem=vector_sends.at[kind, at], recv_sem=vector_recvs.at[kind, at],
+                    device_id=partner(where, hop), device_id_type=MESH,
+                )
+            )
+        return copies
+
+    def vector_advance(kind, action):
+        source, target = [(feature_parts, feature_inbox), (sample_parts, sample_inbox)][kind]
         if action > 0:
-            vector_exchange(action - 1).wait()
-            vector_parts[action] = vector_parts[action - 1] + vector_inbox[action - 1]
-        if action < bits:
-            vector_exchange(action).start()
+            for copy in vector_exchanges(kind, action - 1):
+                copy.wait()
+            where = vector_order[action - 1]
+            first = vector_hops[action - 1] + action - 1
+            target[first + digit(where)] = source[action - 1]
+            total = target[first]
+            for other in range(1, 2 ** where[2]):
+                total = total + target[first + other]
+            source[action] = total
+        if action < len(vector_order):
+            for copy in vector_exchanges(kind, action):
+                copy.start()
         else:
-            vectors_ref[...] = vector_parts[bits]
+            rows = source.shape[1]
+            first = kind * feature_parts.shape[1]
+            vectors_ref[first:first + rows] = source[action]
 
     @pl.when(step == 0)
     def _():
         barrier = pltpu.get_barrier_semaphore()
-        for where in orders[0]:
-            pl.semaphore_signal(
-                barrier, inc=1, device_id=partner(*where), device_id_type=MESH
-            )
+        for where in vector_order:
+            for hop in range(1, 2 ** where[2]):
+                pl.semaphore_signal(
+                    barrier, inc=1, device_id=partner(where, hop), device_id_type=MESH
+                )
         for job in range(feature_jobs):
             load(job).start()
         turned[...] = project[...].T
         project_sum[...] = jnp.zeros_like(project_sum)
         output_sum[...] = jnp.zeros_like(output_sum)
         vector_grad[...] = jnp.zeros_like(vector_grad)
-        pl.semaphore_wait(barrier, bits)
-
+        feature_parts[0] = feature_vectors[...]
+        pl.semaphore_wait(barrier, vector_hops[-1])
+        vector_advance(0, 0)
+
+    for action in range(1, len(vector_order) + 1):
+        @pl.when(step == action)
+        def _():
+            vector_advance(0, action)
+
+    pl.when(step < local)(
+        lambda: sample_backward_attention(
+            step, feature_tick, inputs_ref, mask_ref, gain_ref, shift_ref, output_w, saved_ref,
+            mixed_ref, log_ref, grad_ref, project_sum, output_sum, vector_grad, packed_all,
+        )
+    )
+
+    @pl.when(step == local - 1)
+    def _():
+        width = project_sum.shape[1]
+        sums = [project_sum.at[part * width:(part + 1) * width] for part in range(3)]
+        per_column = size // 2
+        for piece, total in enumerate(sums + [output_sum]):
+            job, first = divmod(piece * width // TILE, per_column)
+            for column in range(width // LANES):
+                lane, inner = divmod(column, width // LANES // 2)
+                begin = inner * per_column + first
+                parts[feature_jobs + job, lane, begin:begin + width // TILE] = total[
+                    :, column * LANES:(column + 1) * LANES
+                ].astype(BF).reshape(width // TILE, TILE, LANES)
+
+    @pl.when(step >= local)
+    def _():
+        feature_tick(0)
+        sample_tick()
+        samples, width = inputs_ref.shape[1:]
+        hat, inverse = normalize(inputs_ref[0].astype(F32))
+        grad_normed = dot(packed_all[step - local], turned[...], 0, 0)
+        grad_rows, grad_gain, grad_shift = normalize_back(grad_normed, gain_ref[...], hat, inverse)
+        stream = grad_ref[...].reshape(samples, width).astype(F32)
+        input_grad_ref[0] = (stream + grad_rows).astype(BF)
+        vector_grad[0:1, :] += grad_gain
+        vector_grad[1:2, :] += grad_shift
+        feature_tick(1)
+
+    @pl.when(step == steps - 1)
+    def _():
+        sample_parts[0] = vector_grad[...]
+        vector_advance(1, 0)
+        for at in range(2 * local, 2 * local + feature_jobs + sample_jobs + last + 1):
+            for tick in range(TICKS * at, TICKS * (at + 1)):
+                for action in reversed(range(last + 1)):
+                    job = tick - offsets[action]
+                    if 0 <= job < feature_jobs:
+                        advance(action, job, True)
+            for action in reversed(range(last + 1)):
+                job = at - local - action
+                if 0 <= job < sample_jobs:
+                    advance(action, feature_jobs + job, False)
+            if 0 < at - 2 * local < len(vector_order) + 1:
+                vector_advance(1, at - 2 * local)
+        for job in range(feature_jobs + sample_jobs):
+            store(job).wait()
+
+
+def sample_backward_attention(
+    step, feature_tick, inputs_ref, mask_ref, gain_ref, shift_ref, output_w, saved_ref,
+    mixed_ref, log_ref, grad_ref, project_sum, output_sum, vector_grad, packed_all,
+):
+    packed_grad = packed_all.at[step]
     samples, width = inputs_ref.shape[1:]
     low_grad = grad_ref[...].reshape(samples, width)
     output_sum[...] += dot(mixed_ref[0], low_grad, 1, 0)
@@ -346,7 +473,7 @@
             first = head * HEAD
             done = odd * (width // PAIR) + pair
             if done % (HEADS // TICKS) == 0:
-                tick(done // (HEADS // TICKS))
+                feature_tick(done // (HEADS // TICKS))
             lanes = slice(pair * PAIR, (pair + 1) * PAIR)
             query_rows = saved_ref[0, 0, first:first + HEAD, :]
             value_rows = saved_ref[0, 2, first:first + HEAD, :]
@@ -374,49 +501,10 @@
             packed_grad[first:first + HEAD, :] = (
                 dot(key_rows, low_scores, 1, 0) * SCALE
             ).astype(BF)
-    hat, inverse = normalize(inputs_ref[0].astype(F32))
+    hat, _ = normalize(inputs_ref[0].astype(F32))
     normed = (hat * gain_ref[...] + shift_ref[...]).astype(BF)
     project_sum[...] += dot(packed_grad[...], normed, 1, 0)
-    grad_normed = dot(packed_grad[...], turned[...], 0, 0)
-    grad_rows, grad_gain, grad_shift = normalize_back(grad_normed, gain_ref[...], hat, inverse)
-    stream = low_grad.astype(F32)
-    input_grad_ref[0] = (stream + grad_rows).astype(BF)
-    vector_grad[0:1, :] += grad_gain
-    vector_grad[1:2, :] += grad_shift
-    vector_grad[2:3, :] += jnp.sum(stream, axis=0, keepdims=True)
-
-    @pl.when(step == steps - 1)
-    def _():
-        vector_parts[0] = jnp.concatenate([feature_vectors[...], vector_grad[...]], axis=0)
-        vector_advance(0)
-        sums = [project_sum.at[part * width:(part + 1) * width] for part in range(3)]
-        per_column = parts.shape[2] // 2
-        for piece, total in enumerate(sums + [output_sum]):
-            job, first = divmod(piece * width // TILE, per_column)
-            for column in range(width // LANES):
-                lane, inner = divmod(column, width // LANES // 2)
-                begin = inner * per_column + first
-                parts[feature_jobs + job, lane, begin:begin + width // TILE] = total[
-                    :, column * LANES:(column + 1) * LANES
-                ].astype(BF).reshape(width // TILE, TILE, LANES)
-        vector_at = 1
-        for at in range(steps, first_sample + sample_jobs + offsets[-1] // TICKS):
-            for point in range(TICKS):
-                for action in reversed(range(2 * bits + 1)):
-                    slot = at - offsets[action] // TICKS
-                    if offsets[action] % TICKS != point:
-                        continue
-                    if 0 <= slot < feature_jobs:
-                        advance(action, slot, True)
-                    if 0 <= slot - first_sample < sample_jobs:
-                        advance(action, feature_jobs + slot - first_sample, False)
-                if vector_at <= bits:
-                    vector_advance(vector_at)
-                    vector_at += 1
-        for late in range(vector_at, bits + 1):
-            vector_advance(late)
-        for job in range(feature_jobs + sample_jobs):
-            store(job).wait()
+    vector_grad[2:3, :] += jnp.sum(low_grad.astype(F32), axis=0, keepdims=True)
 
 
 def finish_kernel(
@@ -771,7 +859,10 @@
     job_rows = 2 * size * TILE // columns
     feature_jobs, sample_jobs = (count * width // job_rows for count in pieces_in)
     jobs = feature_jobs + sample_jobs
-    bits = (peers * tasks).bit_length() - 1
+    *orders, vector_order = axis_orders(peers, tasks)
+    lane_hops = hop_offsets(orders[0] + orders[0][::-1])[-1]
+    vector_hops = hop_offsets(vector_order)[-1]
+    vector_stages = len(vector_order)
 
     position = lax.iota(jnp.int32, samples)
     visible = (position < context[0]) & (sample_mask[0] == 1)
@@ -844,22 +935,36 @@
         up_weight, up_bias.reshape(chunks, 1, chunk), down_chunks, row(down_bias),
     )
     stack_shape = (jobs, 2, size, TILE, LANES)
+    again = lambda *tail: lambda step: (step % local,) + tail
+    early = lambda *tail: lambda step: (jnp.minimum(step, local - 1),) + tail
     input_grad, summed, vectors = call(
-        functools.partial(sample_backward_kernel, peers, tasks, feature_jobs, sample_jobs), local,
-        [
-            token_spec, whole((samples, 1)), line, line, whole((width, 3 * width)), square,
-            saved_spec, token_spec, log_spec, peer_spec, whole((16, width)), anywhere,
-        ],
-        [token_spec, anywhere, whole_out((24, width))],
+        functools.partial(sample_backward_kernel, peers, tasks, feature_jobs, sample_jobs),
+        2 * local,
+        [
+            pl.BlockSpec((1, samples, width), again(0, 0)), whole((samples, 1)), line, line,
+            whole((width, 3 * width)), square,
+            pl.BlockSpec((1, 3, samples, width), early(0, 0, 0)),
+            pl.BlockSpec((1, samples, width), early(0, 0)),
+            pl.BlockSpec((1, HEADS, samples), early(0, 0)),
+            pl.BlockSpec((peers, 1, share, width), lambda step: (0, step % local, 0, 0)),
+            whole((16, width)), anywhere,
+        ],
+        [
+            pl.BlockSpec((1, samples, width), lambda step: (jnp.maximum(step - local, 0), 0, 0)),
+            anywhere, whole_out((24, width)),
+        ],
         [((local, samples, width), BF), (stack_shape, BF), ((24, width), F32)],
         [
             pltpu.VMEM((3 * width, width), F32), pltpu.VMEM((width, width), F32),
-            pltpu.VMEM((8, width), F32),
-            pltpu.VMEM((3 * width, width), BF), pltpu.VMEM((3 * width, samples), BF),
+            pltpu.VMEM((8, width), F32), pltpu.VMEM((3 * width, width), BF),
+            pltpu.VMEM((local, 3 * width, samples), BF),
             pltpu.VMEM(stack_shape, BF), pltpu.VMEM(stack_shape, BF), pltpu.VMEM(stack_shape, BF),
-            pltpu.VMEM((bits + 1, 24, width), F32), pltpu.VMEM((bits, 24, width), F32),
-            sems((feature_jobs,)), sems((jobs,)), sems((2, 2, 2 * bits)), sems((2, 2, 2 * bits)),
-            sems((bits,)), sems((bits,)),
+            pltpu.VMEM((vector_stages + 1, 16, width), F32),
+            pltpu.VMEM((vector_hops + vector_stages, 16, width), F32),
+            pltpu.VMEM((vector_stages + 1, 8, width), F32),
+            pltpu.VMEM((vector_hops + vector_stages, 8, width), F32),
+            sems((feature_jobs,)), sems((jobs,)), sems((jobs, 2, lane_hops)), sems((jobs, 2, lane_hops)),
+            sems((2, vector_hops)), sems((2, vector_hops)),
         ],
         "sample_backward", 110_000_000_000, 50_000_000, 2,
     )(

time: 476 us -> 430 us (0.903)
  Pallas kernels: 467 us -> 417 us
    pallas_call x1, Pallas kernels: 170 us -> 123 us  [body(): call(functools.partial(sample_backward_kernel, peers, tasks, feature_jobs...]
where the time goes in v3:
time: 430 us; the launch traced here: 423 us
  Pallas kernels  417 us (97%)
    pallas_call x1, Pallas kernels, body(): call(functools.partial(feature_kernel, peers), share // group, [block_spe...  213 us
    pallas_call x1, Pallas kernels, body(): call(functools.partial(sample_backward_kernel, peers, tasks, feature_jobs...  123 us
    pallas_call x1, Pallas kernels, body(): call(functools.partial(sample_forward_kernel, peers), local, [token_spec,...  59.4 us
    pallas_call x1, Pallas kernels, body(): call(functools.partial(finish_kernel, chunks), blocks, [pl.BlockSpec((1,...  21 us

profile of v3, /device:TPU:0, one launch (start us, length us, event | category | flops | bytes accessed | tf_op | source)
XLA Modules:
  0.0 422.9 jit_solution(5881719115038667750)
XLA Ops:
  1.3 0.7 compare_bitcast_fusion
  2.0 0.2 copy.38
  2.2 0.8 fusion.1.mask_ref
  3.0 59.4 %sample_forward.1 = (bf16[8,8,64,512]{3,2,1,0:T(8,128)(2,1)}, bf16[8,3,512,512]{3,2,1,0:T(8,128)(2,1)}, bf16[8,512,512]{2,1,0:T(8,128)(2,1)}, f32[8,8,512]{2,1,0:T(8,128)}) custom-call(bf16[8,512,512]{2,1,0:T(8,128)(2,1)} %bitcast.47, f32[512,1]{1,0:T(8,128)} %fusion.1.mask_ref, f32[1,512]{1,0:T(1,128)} %bitcast.59, f32[1,512]{1,0:T(1,128)} %bitcast.61, ...), custom_call_target="tpu_custom_call" | custom-call | flops 60000002048 | bytes 30000000 | tf_op jit(solution)/shard_map/sample_forward/pallas_call | solution.py:881
  62.4 213.3 %feature_block.1 = (bf16[8,8,64,512]{3,2,1,0:T(8,128)(2,1)}, bf16[8,8,64,512]{3,2,1,0:T(8,128)(2,1)}, bf16[6,4,1024,128]{3,2,1,0:T(8,128)(2,1)}, f32[16,512]{1,0:T(8,128)}) custom-call(bf16[64,64,512]{2,1,0:T(8,128)(2,1)} %bitcast.64, bf16[8,512,512]{2,1,0:T(8,128)(2,1)} %bitcast.46, f32[1,512]{1,0:T(1,128)} %bitcast.53, f32[1,512]{1,0:T(1,128)} %bitcast.54, ...), custom_call_target="tpu_custom_call" | custom-call | flops 130000003072 | bytes 40000000 | tf_op jit(solution)/shard_map/feature_block/pallas_call | solution.py:901
  275.7 123.1 %sample_backward.1 = (bf16[8,512,512]{2,1,0:T(8,128)(2,1)}, bf16[8,2,128,16,128]{4,3,2,1,0:T(8,128)(2,1)}, f32[24,512]{1,0:T(8,128)}) custom-call(bf16[8,512,512]{2,1,0:T(8,128)(2,1)} %bitcast.48, f32[512,1]{1,0:T(8,128)} %fusion.1.mask_ref, f32[1,512]{1,0:T(1,128)} %bitcast.60, f32[1,512]{1,0:T(1,128)} %bitcast.62, bf16[512,1536]{1,0:T(8,128)(2,1)} %project.5, ...), custom_call_target="tpu_custom_call" | custom-call | flops 109999996928 | bytes 50000000 | tf_op jit(solution)/shard_map/sample_backward/pallas_call | solution.py:940
  398.8 0.7 slice_bitcast_fusion
  399.5 1.6 fusion.2
  401.1 0.6 copy.39
  401.7 21.0 %finish.1 = (f32[512,2048]{1,0:T(8,128)}, f32[2048,512]{1,0:T(8,128)}, f32[512,1536]{1,0:T(8,128)}, f32[512,512]{1,0:T(8,128)}, f32[512,1536]{1,0:T(8,128)}, /*i...) custom-call(bf16[8,4,1024,128]{3,2,1,0:T(8,128)(2,1)} %bitcast.34, ...), custom_call_target="tpu_custom_call" | custom-call | bytes 46000000 | tf_op jit(solution)/shard_map/finish/pallas_call | solution.py:993

commit v4 on v3

--- a/solution.py
+++ b/solution.py
@@ -508,31 +508,73 @@
 
 
 def finish_kernel(
-    chunks, summed_ref, input_ref, result_ref,
+    chunks, summed, inputs, results, vectors_ref,
     up_grad, down_grad, feature_project, feature_output, sample_project, sample_output,
-    input_grad_ref, output_ref,
+    input_grad, output, hidden_ref, *refs,
 ):
-    step = pl.program_id(0)
-    _, rows, width = output_ref.shape
-    input_grad_ref[...] = input_ref[...].astype(F32)
-    output_ref[...] = result_ref[...].reshape(1, rows, width)
-    bounds = [
-        (up_grad, chunks, False), (down_grad, chunks, False), (feature_project, 3, True),
-        (feature_output, 1, False), (sample_project, 3, True), (sample_output, 1, False),
+    *vector_refs, piece_in, piece_out, token_in, token_out, result_box, loads, stores = refs
+    pieces, columns, width, _ = piece_in.shape
+    local = token_in.shape[0]
+    per_job = summed.shape[2] // width
+
+    def load_piece(index):
+        part = pl.ds(index % per_job * width, width)
+        return pltpu.make_async_copy(
+            summed.at[index // per_job, :, part], piece_in.at[index], loads.at[0, index]
+        )
+
+    def load_token(index):
+        return pltpu.make_async_copy(inputs.at[index], token_in.at[index], loads.at[1, index])
+
+    def load_result(index):
+        return pltpu.make_async_copy(results.at[:, index], result_box.at[index], loads.at[2, index])
+
+    across = lambda target, count: [
+        (target.at[:, pl.ds(at * width, width)], count == 3) for at in range(count)
     ]
-    start = 0
-    for target, count, turn in bounds:
-        @pl.when((step >= start) & (step < start + count))
-        def _():
-            for column in range(width // LANES):
-                piece = summed_ref[0, column].astype(F32)
-                span = slice(column * LANES, (column + 1) * LANES)
-                if turn:
-                    target[span, :] = piece.T
-                else:
-                    target[:, span] = piece
-
-        start += count
+    down = lambda target, count: [
+        (target.at[pl.ds(at * width, width)], False) for at in range(count)
+    ]
+    places = (
+        across(up_grad, chunks) + down(down_grad, chunks) + across(feature_project, 3)
+        + down(feature_output, 1) + across(sample_project, 3) + down(sample_output, 1)
+    )
+    copies = []
+    for index in range(pieces):
+        load_piece(index).start()
+        if index < local:
+            load_token(index).start()
+            load_result(index).start()
+    for index, target in enumerate(vector_refs):
+        first = index if index < 6 else index + 10
+        target[...] = vectors_ref[first:first + 1, :]
+    for index in range(hidden_ref.shape[1] // width):
+        hidden_ref[:, index * width:(index + 1) * width] = vectors_ref[8 + index:9 + index, :]
+    for index, (target, turn) in enumerate(places):
+        load_piece(index).wait()
+        for column in range(columns):
+            piece = piece_in[index, column].astype(F32)
+            span = slice(column * LANES, (column + 1) * LANES)
+            if turn:
+                piece_out[index, span, :] = piece.T
+            else:
+                piece_out[index, :, span] = piece
+        copies.append(pltpu.make_async_copy(piece_out.at[index], target, stores.at[0, index]))
+        copies[-1].start()
+        if index < local:
+            load_token(index).wait()
+            token_out[index] = token_in[index].astype(F32)
+            copies.append(
+                pltpu.make_async_copy(token_out.at[index], input_grad.at[index], stores.at[1, index])
+            )
+            copies[-1].start()
+            load_result(index).wait()
+            copies.append(
+                pltpu.make_async_copy(result_box.at[index], output.at[index], stores.at[2, index])
+            )
+            copies[-1].start()
+    for copy in copies:
+        copy.wait()
 
 
 def to_groups(block_ref, spare):
@@ -973,57 +1015,34 @@
         feature_stacked.reshape((feature_jobs,) + stack_shape[1:]),
     )
     blocks = sum(pieces_in)
-    per_job = job_rows // width
-    per_feature = blocks // local
-    rows = samples // per_feature
-    token_rows = pl.BlockSpec(
-        (1, rows, width), lambda step: (step // per_feature, step % per_feature, 0)
-    )
-
-    def piece_out(shape, start, count, across):
-        def place(step):
-            at = jnp.clip(step - start, 0, count - 1)
-            return (0, at) if across else (at, 0)
-
-        return pl.BlockSpec(shape, place)
-
+    once = lambda shape: pl.BlockSpec(shape, lambda step: (0,) * len(shape))
     (
         up_grad, down_grad, feature_project_grad, feature_output_grad,
-        sample_project_grad, sample_output_grad, input_grad, output,
+        sample_project_grad, sample_output_grad, input_grad, output, hidden_grad, *vectors,
     ) = call(
-        functools.partial(finish_kernel, chunks), blocks,
-        [
-            pl.BlockSpec(
-                (1, columns, width, LANES), lambda step: (step // per_job, 0, step % per_job, 0)
-            ),
-            token_rows,
-            pl.BlockSpec(
-                (peers // per_feature, 1, share, width),
-                lambda step: (step % per_feature, step // per_feature, 0, 0),
-            ),
-        ],
-        [
-            piece_out((width, chunk), 0, chunks, True),
-            piece_out((chunk, width), chunks, chunks, False),
-            piece_out((width, width), 2 * chunks, 3, True),
-            piece_out((width, width), 2 * chunks + 3, 1, True),
-            piece_out((width, width), 2 * chunks + 4, 3, True),
-            piece_out((width, width), 2 * chunks + 7, 1, True),
-            token_rows, token_rows,
-        ],
+        functools.partial(finish_kernel, chunks), 1,
+        [anywhere, anywhere, anywhere, whole((24, width))],
+        [anywhere] * 8 + [once((1, hidden))] + [once((1, width))] * 9,
         [
             ((width, hidden), F32), ((hidden, width), F32), ((width, 3 * width), F32),
             ((width, width), F32), ((width, 3 * width), F32), ((width, width), F32),
-            ((local, samples, width), F32), ((local, samples, width), BF),
+            ((local, samples, width), F32), ((local, peers, share, width), BF), ((1, hidden), F32),
+        ] + [((1, width), F32)] * 9,
+        [
+            pltpu.VMEM((blocks, columns, width, LANES), BF), pltpu.VMEM((blocks, width, width), F32),
+            pltpu.VMEM((local, samples, width), BF), pltpu.VMEM((local, samples, width), F32),
+            pltpu.VMEM((local, peers, share, width), BF), sems((3, blocks)), sems((3, blocks)),
         ],
-        [], "finish", 0, 46_000_000,
-    )(summed.reshape(jobs, columns, job_rows, LANES), input_grad, result_returned)
+        "finish", 0, 46_000_000,
+    )(summed.reshape(jobs, columns, job_rows, LANES), input_grad, result_returned, vectors)
+    output = output.reshape(local, samples, width)
+    vectors = [vector.reshape(width) for vector in vectors]
     return (
         output[None], input_grad[None],
-        vectors[16], vectors[17], sample_project_grad, sample_output_grad,
-        vectors[18], vectors[0], vectors[1], feature_project_grad,
+        vectors[6], vectors[7], sample_project_grad, sample_output_grad,
+        vectors[8], vectors[0], vectors[1], feature_project_grad,
         feature_output_grad, vectors[2], vectors[3], vectors[4],
-        up_grad, vectors[8:8 + hidden // width].reshape(hidden), down_grad, vectors[5],
+        up_grad, hidden_grad.reshape(hidden), down_grad, vectors[5],
     )
 
 

time: 430 us -> 423 us (0.984)
  Pallas kernels: 417 us -> 412 us
where the time goes in v4:
time: 423 us; the launch traced here: 416 us
  Pallas kernels  412 us (97%)
    pallas_call x1, Pallas kernels, body(): call(functools.partial(feature_kernel, peers), share // group, [block_spe...  212 us
    pallas_call x1, Pallas kernels, body(): call(functools.partial(sample_backward_kernel, peers, tasks, feature_jobs...  123 us
    pallas_call x1, Pallas kernels, body(): call(functools.partial(sample_forward_kernel, peers), local, [token_spec,...  59.4 us
    pallas_call x1, Pallas kernels, body(): call(functools.partial(finish_kernel, chunks), 1, [anywhere, anywhere, an...  17.8 us

profile of v4, /device:TPU:0, one launch (start us, length us, event | category | flops | bytes accessed | tf_op | source)
XLA Modules:
  0.0 415.6 jit_solution(394810605064215322)
XLA Ops:
  1.3 0.7 compare_bitcast_fusion
  2.0 0.2 copy.38
  2.2 0.8 fusion.1.mask_ref
  3.0 59.4 %sample_forward.1 = (bf16[8,8,64,512]{3,2,1,0:T(8,128)(2,1)}, bf16[8,3,512,512]{3,2,1,0:T(8,128)(2,1)}, bf16[8,512,512]{2,1,0:T(8,128)(2,1)}, f32[8,8,512]{2,1,0:T(8,128)}) custom-call(bf16[8,512,512]{2,1,0:T(8,128)(2,1)} %bitcast.35, f32[512,1]{1,0:T(8,128)} %fusion.1.mask_ref, f32[1,512]{1,0:T(1,128)} %bitcast.48, f32[1,512]{1,0:T(1,128)} %bitcast.50, ...), custom_call_target="tpu_custom_call" | custom-call | flops 60000002048 | bytes 30000000 | tf_op jit(solution)/shard_map/sample_forward/pallas_call | solution.py:923
  62.4 212.1 %feature_block.1 = (bf16[8,8,64,512]{3,2,1,0:T(8,128)(2,1)}, bf16[8,8,64,512]{3,2,1,0:T(8,128)(2,1)}, bf16[6,4,1024,128]{3,2,1,0:T(8,128)(2,1)}, f32[16,512]{1,0:T(8,128)}) custom-call(bf16[64,64,512]{2,1,0:T(8,128)(2,1)} %bitcast.62, bf16[8,512,512]{2,1,0:T(8,128)(2,1)} %bitcast.34, f32[1,512]{1,0:T(1,128)} %bitcast.42, f32[1,512]{1,0:T(1,128)} %bitcast.43, ...), custom_call_target="tpu_custom_call" | custom-call | flops 130000003072 | bytes 40000000 | tf_op jit(solution)/shard_map/feature_block/pallas_call | solution.py:943
  274.5 123.0 %sample_backward.1 = (bf16[8,512,512]{2,1,0:T(8,128)(2,1)}, bf16[8,2,128,16,128]{4,3,2,1,0:T(8,128)(2,1)}, f32[24,512]{1,0:T(8,128)}) custom-call(bf16[8,512,512]{2,1,0:T(8,128)(2,1)} %bitcast.36, f32[512,1]{1,0:T(8,128)} %fusion.1.mask_ref, f32[1,512]{1,0:T(1,128)} %bitcast.49, f32[1,512]{1,0:T(1,128)} %bitcast.51, bf16[512,1536]{1,0:T(8,128)(2,1)} %project.5, ...), custom_call_target="tpu_custom_call" | custom-call | flops 109999996928 | bytes 50000000 | tf_op jit(solution)/shard_map/sample_backward/pallas_call | solution.py:982
  397.5 17.8 %finish.1 = (f32[512,2048]{1,0:T(8,128)}, f32[2048,512]{1,0:T(8,128)}, f32[512,1536]{1,0:T(8,128)}, f32[512,512]{1,0:T(8,128)}, f32[512,1536]{1,0:T(8,128)}, /*i...) custom-call(bf16[8,4,1024,128]{3,2,1,0:T(8,128)(2,1)} %bitcast.32, ...), custom_call_target="tpu_custom_call" | custom-call | bytes 46000000 | tf_op jit(solution)/shard_map/finish/pallas_call | solution.py:1022

commit v5 on v4

--- a/solution.py
+++ b/solution.py
@@ -607,8 +607,8 @@
     peers,
     stream_ref, cotangent_hbm, gain_ref, shift_ref, project, output_w,
     bias_ref, dense_gain_ref, dense_shift_ref, up_ref, up_bias_ref, down_ref, down_bias_ref,
-    results_ref, grads_ref, stacked_ref, vectors_ref,
-    vector_grad, hidden_grad, project_sum, output_sum, up_sum, down_sum, turned, spare, query_t, keys_s, value_t, mixed_t, logs,
+    results_ref, grads_ref, stacked_hbm, vectors_ref,
+    stacked_ref, stack_sem, vector_grad, hidden_grad, project_sum, output_sum, up_sum, down_sum, turned, spare, query_t, keys_s, value_t, mixed_t, logs,
     packed_grad, cotangents, result_box, grad_box,
     cotangent_sends, cotangent_recvs, result_sends, grad_sends, result_recvs, grad_recvs, own_sems,
 ):
@@ -839,6 +839,8 @@
                 stacked_ref[job, column, first:first + width, :] = total[
                     :, column * LANES:(column + 1) * LANES
                 ].astype(BF)
+        stacking = pltpu.make_async_copy(stacked_ref, stacked_hbm, stack_sem)
+        stacking.start()
         for send in cotangent_moves(step):
             send.wait_send()
         drain(result_moves(step, slot))
@@ -852,6 +854,7 @@
             source = (me + peers - hop) % peers
             arrived(results_ref.at[source], result_recvs.at[hop])
             arrived(grads_ref.at[source], grad_recvs.at[hop])
+        stacking.wait()
 
 
 def whole(shape):
@@ -948,14 +951,14 @@
             whole((chunks, chunk, width)), line,
         ],
         [
-            anywhere, anywhere, whole_out((feature_jobs, columns, job_rows, LANES)),
-            whole_out((16, width)),
+            anywhere, anywhere, anywhere, whole_out((16, width)),
         ],
         [
             (peer_shape, BF), (peer_shape, BF),
             ((feature_jobs, columns, job_rows, LANES), BF), ((16, width), F32),
         ],
         [
+            pltpu.VMEM((feature_jobs, columns, job_rows, LANES), BF), sems,
             pltpu.VMEM((8, width), F32), pltpu.VMEM((chunks, 1, chunk), F32),
             pltpu.VMEM((3 * width, width), F32), pltpu.VMEM((width, width), F32),
             pltpu.VMEM((chunks, width, chunk), F32), pltpu.VMEM((chunks, chunk, width), F32),

time: 423 us -> 421 us (level)
  no operation moved by 1% of the time
where the time goes in v5:
time: 421 us; the launch traced here: 414 us
  Pallas kernels  410 us (97%)
    pallas_call x1, Pallas kernels, body(): call(functools.partial(feature_kernel, peers), share // group, [block_spe...  210 us
    pallas_call x1, Pallas kernels, body(): call(functools.partial(sample_backward_kernel, peers, tasks, feature_jobs...  123 us
    pallas_call x1, Pallas kernels, body(): call(functools.partial(sample_forward_kernel, peers), local, [token_spec,...  59.4 us
    pallas_call x1, Pallas kernels, body(): call(functools.partial(finish_kernel, chunks), 1, [anywhere, anywhere, an...  17.8 us

profile of v5, /device:TPU:0, one launch (start us, length us, event | category | flops | bytes accessed | tf_op | source)
XLA Modules:
  0.0 413.5 jit_solution(9714381928933033016)
XLA Ops:
  1.3 0.7 compare_bitcast_fusion
  2.0 0.2 copy.38
  2.2 0.8 fusion.1.mask_ref
  3.0 59.4 %sample_forward.1 = (bf16[8,8,64,512]{3,2,1,0:T(8,128)(2,1)}, bf16[8,3,512,512]{3,2,1,0:T(8,128)(2,1)}, bf16[8,512,512]{2,1,0:T(8,128)(2,1)}, f32[8,8,512]{2,1,0:T(8,128)}) custom-call(bf16[8,512,512]{2,1,0:T(8,128)(2,1)} %bitcast.35, f32[512,1]{1,0:T(8,128)} %fusion.1.mask_ref, f32[1,512]{1,0:T(1,128)} %bitcast.48, f32[1,512]{1,0:T(1,128)} %bitcast.50, ...), custom_call_target="tpu_custom_call" | custom-call | flops 60000002048 | bytes 30000000 | tf_op jit(solution)/shard_map/sample_forward/pallas_call | solution.py:926
  62.4 210.1 %feature_block.1 = (bf16[8,8,64,512]{3,2,1,0:T(8,128)(2,1)}, bf16[8,8,64,512]{3,2,1,0:T(8,128)(2,1)}, bf16[6,4,1024,128]{3,2,1,0:T(8,128)(2,1)}, f32[16,512]{1,0:T(8,128)}) custom-call(bf16[64,64,512]{2,1,0:T(8,128)(2,1)} %bitcast.62, bf16[8,512,512]{2,1,0:T(8,128)(2,1)} %bitcast.34, f32[1,512]{1,0:T(1,128)} %bitcast.42, f32[1,512]{1,0:T(1,128)} %bitcast.43, ...), custom_call_target="tpu_custom_call" | custom-call | flops 130000003072 | bytes 40000000 | tf_op jit(solution)/shard_map/feature_block/pallas_call | solution.py:946
  272.5 122.9 %sample_backward.1 = (bf16[8,512,512]{2,1,0:T(8,128)(2,1)}, bf16[8,2,128,16,128]{4,3,2,1,0:T(8,128)(2,1)}, f32[24,512]{1,0:T(8,128)}) custom-call(bf16[8,512,512]{2,1,0:T(8,128)(2,1)} %bitcast.36, f32[512,1]{1,0:T(8,128)} %fusion.1.mask_ref, f32[1,512]{1,0:T(1,128)} %bitcast.49, f32[1,512]{1,0:T(1,128)} %bitcast.51, bf16[512,1536]{1,0:T(8,128)(2,1)} %project.5, ...), custom_call_target="tpu_custom_call" | custom-call | flops 109999996928 | bytes 50000000 | tf_op jit(solution)/shard_map/sample_backward/pallas_call | solution.py:985
  395.4 17.8 %finish.1 = (f32[512,2048]{1,0:T(8,128)}, f32[2048,512]{1,0:T(8,128)}, f32[512,1536]{1,0:T(8,128)}, f32[512,512]{1,0:T(8,128)}, f32[512,1536]{1,0:T(8,128)}, /*i...) custom-call(bf16[8,4,1024,128]{3,2,1,0:T(8,128)(2,1)} %bitcast.32, ...), custom_call_target="tpu_custom_call" | custom-call | bytes 46000000 | tf_op jit(solution)/shard_map/finish/pallas_call | solution.py:1025
